TPU v7x, 512 devices: a whole 4x8x8 slice. The times are simulated.
512 devices in a mesh: seq: 32 (over z_hi, y), tensor: 8 (over x, z_lo), group: 2 (over core).
Axes of the slice: x: 4, y: 8, z: 8 (z_hi: 4, z_lo: 2; z = z_hi * 2 + z_lo), core: 2. Of those that a mesh axis runs over, the one named last changes fastest.
Arguments:
- prefill_queries: bfloat16 [512, 8192], P(None, 'tensor'), may hold values from -6 to 6
- cached_keys: bfloat16 [65536, 1024], P(('seq', 'group'), 'tensor'), may hold values from -6 to 6
- cached_values: bfloat16 [65536, 1024], P(('seq', 'group'), 'tensor'), may hold values from -6 to 6
- span_keys: bfloat16 [512, 1024], P(('seq', 'group'), 'tensor'), may hold values from -6 to 6
- span_values: bfloat16 [512, 1024], P(('seq', 'group'), 'tensor'), may hold values from -6 to 6
- out_weight: bfloat16 [8192, 8192], P('tensor', 'seq'), may hold values from -0.0625 to 0.0625
- decode_queries: bfloat16 [4, 32, 8192], P(None, 'group', 'tensor'), may hold values from -6 to 6
- decode_keys: bfloat16 [32, 8192, 1024], P('group', 'seq', 'tensor'), may hold values from -6 to 6
- decode_values: bfloat16 [32, 8192, 1024], P('group', 'seq', 'tensor'), may hold values from -6 to 6
- new_keys: bfloat16 [4, 32, 1024], P(None, 'group', 'tensor'), may hold values from -6 to 6
- new_values: bfloat16 [4, 32, 1024], P(None, 'group', 'tensor'), may hold values from -6 to 6
- request_lengths: int32 [32], replicated, may hold values from 1 to 8192
- row_requests: int32 [32], P('group'), may hold values from 0 to 31
- block_table: int32 [128, 1], replicated, may hold values from 0 to 63; in each aligned block of 128 rows (0 to 127, 128 to 255, ...) at most 4 rows name the same one
Outputs:
- prefill_out: bfloat16 [512, 8192], P('group', ('seq', 'tensor'))
- decode_out: bfloat16 [4, 32, 8192], P(None, 'group', ('seq', 'tensor'))
- landed_keys: bfloat16 [64, 4, 4, 1024], P(('seq', 'group'), None, None, 'tensor')
- landed_values: bfloat16 [64, 4, 4, 1024], P(('seq', 'group'), None, None, 'tensor')
Inputs may be any that keep to these rules, and one draw needn't show every extreme that they name: `block_table`: each owner receives at most 4 blocks, and some owner receives exactly 4; every owner receives at least one.
All inputs are finite; a program needn't handle non-finite values.
Results may differ from a plain program's by a relative error of at most 0.0052.
Values may be sent and summed in bfloat16 or wider, within the bound.
No kernel may reach another device: no remote copies, remote signals or barrier semaphores. Data moves between devices by JAX's collectives and lax.ppermute only.
A program may use at most 64 MiB of HBM per device.

v0:
```python
import math

import jax
import jax.numpy as jnp
from jax import lax
from jax.sharding import Mesh
from jax.sharding import PartitionSpec as P

HEADS = 64
KV_HEADS = 8
HEAD = 128
SPAN = 512
BLOCK = 4
SEQ = ("seq_0", "seq_1")
SEQ_GROUP = ("seq_0", "seq_1", "group")
SEQ_TENSOR = ("seq_0", "seq_1", "tensor")


masked_score = -1e30


def from_everyone(shard, axis):
    peers = lax.axis_size(axis)
    return lax.all_to_all(
        jnp.broadcast_to(shard[None], (peers, *shard.shape)), axis, 0, 0, tiled=True
    )


def of_everyone(shard, axis):
    return from_everyone(shard, axis).max(axis=0)


def split_up(shard, dim, peers):
    before, after = (shard.shape[:dim], shard.shape[dim + 1 :])
    return jnp.moveaxis(shard.reshape(*before, peers, -1, *after), dim, 0)


def summed_on_arrival(shard, axis, dim):
    pieces = split_up(shard, dim, lax.axis_size(axis))
    arrived = lax.all_to_all(pieces, axis, split_axis=0, concat_axis=0, tiled=True)
    return arrived.sum(axis=0)


def sum_in_two_steps(shard, axes, dim):
    far, near = axes
    own = summed_on_arrival(split_up(shard, dim, lax.axis_size(far)), near, dim + 1)
    return jnp.sum(lax.all_to_all(own, far, 0, 0, tiled=True), axis=0)


def side_by_side(arrays, axis, dim, along):
    widths = [math.prod(a.shape[along:]) for a in arrays]
    both = jnp.concatenate(
        [a.reshape(*a.shape[:along], w) for a, w in zip(arrays, widths)], axis=along
    )
    result = sum_in_two_steps(both, axis, dim)
    pieces = jnp.split(result, [sum(widths[:k]) for k in range(1, len(widths))], axis=along)
    return tuple(
        (b.reshape(*result.shape[:along], *a.shape[along:]) for a, b in zip(arrays, pieces))
    )


def laid_out(pieces, dim):
    pieces = jnp.moveaxis(pieces, 0, dim)
    shape = pieces.shape
    return pieces.reshape(*shape[:dim], shape[dim] * shape[dim + 1], *shape[dim + 2 :])


def collect(shard, axis, dim):
    pieces = from_everyone(shard, axis)
    return laid_out(pieces, dim)


def filled_up(lines, peers):
    spare = -lines.shape[0] % peers
    if not spare:
        return lines
    return jnp.concatenate([lines, jnp.zeros((spare, *lines.shape[1:]), lines.dtype)])


def sum_by_parts(shard, axes):
    padded = filled_up(shard, lax.axis_size(axes))
    whole = collect(summed_on_arrival(padded, axes, 0), axes, 0)
    return lax.slice_in_dim(whole, 0, len(shard)).reshape(shard.shape)


def together(arrays, axis):
    flat, at, done = (jnp.concatenate([a.reshape(-1) for a in arrays]), 0, [])
    total = sum_by_parts(flat, axis)
    for a in arrays:
        done.append(total[at : at + a.size].reshape(a.shape))
        at += a.size
    return tuple(done)


def sent_together(arrays, axis, dim, along):
    both = jnp.concatenate(arrays, axis=along)
    result, at, done = (summed_on_arrival(both, axis, dim), 0, [])
    for a in arrays:
        done.append(lax.slice_in_dim(result, at, at + a.shape[along], axis=along))
        at += a.shape[along]
    return tuple(done)


def in_one_piece(arrays, axis, dim, along):
    both = jnp.concatenate(arrays, axis=along)
    result, at, done = (lax.all_gather(both, axis, axis=dim, tiled=True), 0, [])
    for a in arrays:
        done.append(lax.slice_in_dim(result, at, at + a.shape[along], axis=along))
        at += a.shape[along]
    return tuple(done)


def prefill_scores(query_rows, keys_one, visible):
    scores = jnp.einsum(
        "qd,kd->qk", query_rows, keys_one, preferred_element_type=jnp.float32
    ) * HEAD ** (-0.5)
    return jnp.where(visible, scores, masked_score)


def body(
    prefill_queries,
    cached_keys,
    cached_values,
    span_keys,
    span_values,
    out_weight,
    decode_queries,
    decode_keys,
    decode_values,
    new_keys,
    new_values,
    request_lengths,
    row_requests,
    block_table,
):
    seq_count = lax.axis_size(SEQ)
    group_count = lax.axis_size("group")
    group_index = lax.axis_index("group")
    owner_index = lax.axis_index(SEQ) * group_count + group_index
    group_size = HEADS // KV_HEADS
    local_heads = prefill_queries.shape[1] // HEAD
    local_groups = cached_keys.shape[1] // HEAD
    span_rows = prefill_queries.shape[0]
    span_local = span_keys.shape[0]
    row_block = span_rows // (seq_count * group_count)
    half_rows = span_rows // group_count
    query_order = jnp.arange(span_rows, dtype=jnp.int32).reshape(group_count, seq_count, row_block)
    query_order = query_order.transpose(1, 0, 2).reshape(span_rows)
    queries = prefill_queries.reshape(group_count, seq_count, row_block, local_heads, HEAD)
    queries = queries.transpose(3, 1, 0, 2, 4).reshape(local_heads, span_rows, HEAD)
    key_rows = jnp.concatenate([cached_keys, span_keys], axis=0).reshape(-1, local_groups, HEAD)
    value_rows = jnp.concatenate([cached_values, span_values], axis=0).reshape(
        -1, local_groups, HEAD
    )
    key_position = jnp.concatenate(
        [
            jnp.full((cached_keys.shape[0],), -1, jnp.int32),
            owner_index * span_local + jnp.arange(span_local, dtype=jnp.int32),
        ]
    )
    visible = key_position[None, :] <= query_order[:, None]
    head_numbers = jnp.arange(local_heads, dtype=jnp.int32)

    def head_peak(inputs):
        query_rows, head_number = inputs
        keys_one = lax.dynamic_index_in_dim(key_rows, head_number // group_size, 1, keepdims=False)
        return jnp.max(prefill_scores(query_rows, keys_one, visible), axis=1)

    row_peak = lax.map(head_peak, (queries, head_numbers))
    row_peak = of_everyone(row_peak, SEQ_GROUP)

    def head_sums(inputs):
        query_rows, head_number, peak_one = inputs
        keys_one = lax.dynamic_index_in_dim(key_rows, head_number // group_size, 1, keepdims=False)
        values_one = lax.dynamic_index_in_dim(
            value_rows, head_number // group_size, 1, keepdims=False
        )
        scores = prefill_scores(query_rows, keys_one, visible)
        weights = jnp.where(visible, jnp.exp(scores - peak_one[:, None]), 0.0)
        weighted = jnp.dot(
            weights.astype(jnp.bfloat16), values_one, preferred_element_type=jnp.float32
        )
        return (weighted, jnp.sum(weights, axis=1))

    weighted, totals = lax.map(head_sums, (queries, head_numbers, row_peak))
    weighted, totals = side_by_side((weighted, totals), (("seq_0", "seq_1"), "group"), 1, 2)
    attention = (weighted / totals[:, :, None]).astype(jnp.bfloat16)
    attention = collect(attention, SEQ, 1)
    attention = attention.transpose(1, 0, 2).reshape(half_rows, local_heads * HEAD)
    span_partial = jnp.dot(attention, out_weight, preferred_element_type=jnp.float32)
    steps = decode_queries.shape[0]
    rows_local = decode_queries.shape[1]
    slots = decode_keys.shape[1]
    score_scale = HEAD ** (-0.5)
    step_queries = decode_queries.reshape(steps, rows_local, local_groups, group_size, HEAD)
    owned_keys = decode_keys.reshape(rows_local, slots, local_groups, HEAD)
    owned_values = decode_values.reshape(rows_local, slots, local_groups, HEAD)
    step_keys = new_keys.reshape(steps, rows_local, local_groups, HEAD)
    step_values = new_values.reshape(steps, rows_local, local_groups, HEAD)
    request_count = request_lengths.shape[0]
    picked = row_requests[:, None] == jnp.arange(request_count, dtype=jnp.int32)[None, :]
    row_length = jnp.sum(jnp.where(picked, request_lengths[None, :], 0), axis=1)
    position = lax.axis_index(SEQ) * slots + jnp.arange(slots, dtype=jnp.int32)
    live = (position[None, :] < row_length[:, None])[:, None, None, None, :]
    causal = (
        jnp.arange(steps, dtype=jnp.int32)[None, :] <= jnp.arange(steps, dtype=jnp.int32)[:, None]
    )
    cache_scores = (
        jnp.einsum(
            "trkgd,rskd->rkgts", step_queries, owned_keys, preferred_element_type=jnp.float32
        )
        * score_scale
    )
    cache_scores = jnp.where(live, cache_scores, masked_score)
    step_scores = (
        jnp.einsum("trkgd,urkd->rkgtu", step_queries, step_keys, preferred_element_type=jnp.float32)
        * score_scale
    )
    step_scores = jnp.where(causal, step_scores, masked_score)
    cache_peak = of_everyone(jnp.max(cache_scores, axis=4), SEQ)
    peak = jnp.maximum(cache_peak, jnp.max(step_scores, axis=4))
    cache_weights = jnp.where(live, jnp.exp(cache_scores - peak[..., None]), 0.0)
    step_weights = jnp.where(causal, jnp.exp(step_scores - peak[..., None]), 0.0)
    cache_sum = jnp.einsum(
        "rkgts,rskd->rkgtd",
        cache_weights.astype(jnp.bfloat16),
        owned_values,
        preferred_element_type=jnp.float32,
    )
    cache_sum, cache_total = together((cache_sum, jnp.sum(cache_weights, axis=4)), SEQ)
    step_sum = jnp.einsum(
        "rkgtu,urkd->rkgtd",
        step_weights.astype(jnp.bfloat16),
        step_values,
        preferred_element_type=jnp.float32,
    )
    decode_total = cache_total + jnp.sum(step_weights, axis=4)
    decoded = ((cache_sum + step_sum) / decode_total[..., None]).astype(jnp.bfloat16)
    decoded = decoded.transpose(3, 0, 1, 2, 4).reshape(steps * rows_local, local_heads * HEAD)
    decode_partial = jnp.dot(decoded, out_weight, preferred_element_type=jnp.float32)
    span_part, decode_part = sent_together((span_partial, decode_partial), "tensor", 1, 0)
    prefill_out = span_part.astype(jnp.bfloat16)
    decode_out = decode_part.astype(jnp.bfloat16).reshape(steps, rows_local, -1)
    gathered_keys, gathered_values = in_one_piece((span_keys, span_values), SEQ_GROUP, 0, 1)
    block_count = SPAN // BLOCK
    most_blocks = 2 * block_count // (seq_count * group_count)
    targets = block_table[:, 0]
    block_order = jnp.arange(block_count, dtype=jnp.int32)
    earlier = (targets[None, :] == targets[:, None]) & (block_order[None, :] < block_order[:, None])
    block_rank = jnp.sum(earlier.astype(jnp.int32), axis=1)
    slot_ids = jnp.arange(most_blocks, dtype=jnp.int32)
    chosen = (targets[None, :] == owner_index) & (block_rank[None, :] == slot_ids[:, None])
    chosen = chosen.astype(jnp.bfloat16)
    landed_keys = jnp.dot(
        chosen, gathered_keys.reshape(block_count, -1), preferred_element_type=jnp.float32
    )
    landed_values = jnp.dot(
        chosen, gathered_values.reshape(block_count, -1), preferred_element_type=jnp.float32
    )
    landed_keys = landed_keys.astype(jnp.bfloat16).reshape(1, most_blocks, BLOCK, -1)
    landed_values = landed_values.astype(jnp.bfloat16).reshape(1, most_blocks, BLOCK, -1)
    return (prefill_out, decode_out, landed_keys, landed_values)


def solution(mesh):
    torus = Mesh(
        mesh.devices.reshape(4, 8, mesh.shape["tensor"], mesh.shape["group"]),
        ("seq_0", "seq_1", "tensor", "group"),
    )
    in_specs = (
        P(None, "tensor"),
        P(SEQ_GROUP, "tensor"),
        P(SEQ_GROUP, "tensor"),
        P(SEQ_GROUP, "tensor"),
        P(SEQ_GROUP, "tensor"),
        P("tensor", SEQ),
        P(None, "group", "tensor"),
        P("group", SEQ, "tensor"),
        P("group", SEQ, "tensor"),
        P(None, "group", "tensor"),
        P(None, "group", "tensor"),
        P(),
        P("group"),
        P(),
    )
    out_specs = (
        P("group", SEQ_TENSOR),
        P(None, "group", SEQ_TENSOR),
        P(SEQ_GROUP, None, None, "tensor"),
        P(SEQ_GROUP, None, None, "tensor"),
    )
    return jax.shard_map(body, mesh=torus, in_specs=in_specs, out_specs=out_specs, check_vma=False)
```

profile of v0, /device:TPU:1, one launch (start us, length us, event | category | flops | bytes accessed | tf_op | source)
XLA Modules:
  0.0 348.6 jit_solution(6777871399052823846)
XLA Ops:
  4.3 16.5 %all-to-all-start.4 = ((f32[32,1,512]{2,1,0:T(1,128)}), f32[32,1,512]{2,1,0:T(1,128)S(1)}, u32[]{:S(2)}, u32[]{:S(2)}) async-start(f32[32,1,512]{2,1,0:T(1,128)} %reshape.280), calls=%async_computation.4 | async-start | bytes 131072 | tf_op jit(solution)/shard_map/all_to_all | solution.py:24
  22.8 11.8 %while.26 = (s32[]{:T(128)}, f32[8,512]{1,0:T(8,128)S(1)}, bf16[8,512,128]{2,1,0:T(8,128)(2,1)}, bf16[1032,1,128]{2,0,1:T(8,128)(2,1)S(1)}, s32[512]{0:T(512)S(1)}, /*index=5*/s32[1032]{0:T(1024)S(1)}, s32[]{:T(128)}, s32[]{:T(128)}) while((s32[]{:T(128)}, f32[8,512]{1,0:T(8,128)S(1)}, bf16[8,512,128]{2,1,0:T(8,128)(2,1)}, ...), condition=%wide.region_2.3_spmd.clone, body=%wide.region_0.2_spmd.clone.sunk | while | flops 137379328 | bytes 408185 | solution.py:169
  22.8 1.4 fusion.82
  35.9 13.3 %all-to-all-start = ((f32[64,8,512]{2,1,0:T(8,128)}), f32[64,8,512]{2,1,0:T(8,128)S(1)}, u32[]{:S(2)}, u32[]{:S(2)}) async-start(f32[64,8,512]{2,1,0:T(8,128)} %broadcast_in_dim.119), calls=%async_computation | async-start | bytes 2097152 | tf_op jit(solution)/shard_map/all_to_all | solution.py:24
  51.2 1.6 reduce.10
  54.5 1.5 fusion.29
  57.1 21.8 %all-to-all-done = f32[64,8,512]{2,1,0:T(8,128)S(1)} async-done(((f32[64,8,512]{2,1,0:T(8,128)}), f32[64,8,512]{2,1,0:T(8,128)S(1)}, u32[]{:S(2)}, u32[]{:S(2)}) %all-to-all-start) | async-done | bytes 1048608 | tf_op jit(solution)/shard_map/all_to_all | solution.py:24
  79.1 24.1 %while.27 = (s32[]{:T(128)}, f32[8,512,128]{2,1,0:T(8,128)}, f32[8,512]{1,0:T(8,128)S(1)}, bf16[8,512,128]{2,1,0:T(8,128)(2,1)}, bf16[1032,1,128]{2,0,1:T(8,128)...) while((s32[]{:T(128)}, f32[8,512,128]{2,1,0:T(8,128)}, ...), condition=%wide.region_6.7_spmd.clone, body=%wide.region_4.6_spmd.clone.sunk | while | flops 274230784 | bytes 3054741 | solution.py:185
  79.1 1.7 fusion.85
  82.1 1.7 fusion.85
  85.1 1.7 fusion.85
  88.1 1.7 fusion.85
  91.2 1.7 fusion.85
  94.2 1.7 fusion.85
  97.2 1.7 fusion.85
  100.2 1.7 fusion.85
  103.2 1.9 concatenate.35
  105.2 2.1 maximum_bitcast_fusion
  107.8 8.8 %all_to_all.45 = f32[2,32,8,8,129]{4,3,1,2,0:T(8,128)} all-to-all(f32[2,32,8,8,129]{4,3,1,2,0:T(8,128)S(1)} %copy.194), channel_id=1, replica_groups=mesh['seq_0'=4,'seq_1'=8,'tensor'=8,'group'=2] {'group'}, dimensions={0} | all-to-all | bytes 4227072 | tf_op jit(solution)/shard_map/all_to_all | solution.py:40
  116.5 6.9 %all-to-all-start.5 = ((f32[32,1,2064]{2,1,0:T(1,128)}), f32[32,1,2064]{2,1,0:T(1,128)S(1)}, u32[]{:S(2)}, u32[]{:S(2)}) async-start(f32[32,1,2064]{2,1,0:T(1,128)} %all_to_all.33), calls=%async_computation.5 | async-start | bytes 557056 | tf_op jit(solution)/shard_map/all_to_all | solution.py:40
  123.4 2.8 reduce_sum.82
  126.2 1.6 copy.196
  127.9 8.3 %all-to-all-done.5 = f32[32,1,2064]{2,1,0:T(1,128)S(1)} async-done(((f32[32,1,2064]{2,1,0:T(1,128)}), f32[32,1,2064]{2,1,0:T(1,128)S(1)}, u32[]{:S(2)}, u32[]{:S(2)}) %all-to-all-start.5) | async-done | bytes 264224 | tf_op jit(solution)/shard_map/all_to_all | solution.py:40
  136.2 6.2 %all-to-all-start.2 = ((f32[32,8,8,129]{3,2,1,0:T(8,128)}), f32[32,8,8,129]{3,2,1,0:T(8,128)S(1)}, u32[]{:S(2)}, u32[]{:S(2)}) async-start(f32[32,8,8,129]{3,2,1,0:T(8,128)} %copy.196), calls=%async_computation.2 | async-start | bytes 4194304 | tf_op jit(solution)/shard_map/all_to_all | solution.py:47
  142.6 66.6 %all-to-all-done.2 = f32[32,8,8,129]{3,2,1,0:T(8,128)S(1)} async-done(((f32[32,8,8,129]{3,2,1,0:T(8,128)}), f32[32,8,8,129]{3,2,1,0:T(8,128)S(1)}, u32[]{:S(2)}, u32[]{:S(2)}) %all-to-all-start.2) | async-done | bytes 1056800 | tf_op jit(solution)/shard_map/all_to_all | solution.py:47
  210.1 8.7 %all-to-all-start.6 = ((f32[32,1,2064]{2,1,0:T(1,128)}), f32[32,1,2064]{2,1,0:T(1,128)S(1)}, u32[]{:S(2)}, u32[]{:S(2)}) async-start(f32[32,1,2064]{2,1,0:T(1,128)} %broadcast_in_dim.130), calls=%async_computation.6 | async-start | bytes 557056 | tf_op jit(solution)/shard_map/all_to_all | solution.py:24
  219.2 11.9 %all-to-all-done.6 = f32[32,1,2064]{2,1,0:T(1,128)S(1)} async-done(((f32[32,1,2064]{2,1,0:T(1,128)}), f32[32,1,2064]{2,1,0:T(1,128)S(1)}, u32[]{:S(2)}, u32[]{:S(2)}) %all-to-all-start.6) | async-done | bytes 264224 | tf_op jit(solution)/shard_map/all_to_all | solution.py:24
  232.1 6.3 %all-to-all-start.3 = ((bf16[32,8,8,128]{3,2,1,0:T(8,128)(2,1)}), bf16[32,8,8,128]{3,2,1,0:T(8,128)(2,1)S(1)}, u32[]{:S(2)}, u32[]{:S(2)}) async-start(bf16[32,8,8,128]{3,2,1,0:T(8,128)(2,1)} %broadcast_in_dim.120), calls=%async_computation.3 | async-start | bytes 1048576 | tf_op jit(solution)/shard_map/all_to_all | solution.py:24
  238.5 87.8 %all_gather.3 = bf16[512,256]{1,0:T(8,128)(2,1)S(1)} all-gather(bf16[8,256]{1,0:T(8,128)(2,1)S(1)} %pad_maximum_fusion.2), channel_id=1, replica_groups=mesh['seq_0'=4,'seq_1'=8,'tensor'=8,'group'=2] {'seq_0','seq_1','group'}, dimensions={0}, use_global_device_ids=true | all-gather | bytes 266240 | tf_op jit(solution)/shard_map/all_gather | solution.py:106
  327.2 4.5 %slice.24 = f32[2064,8,4]{2,1,0:T(8,128)} reshape(f32[32,2064]{1,0:T(8,128)S(1)} %reduce.7) | data formatting | bytes 528384 | tf_op jit(solution)/shard_map/slice | solution.py:90
  335.2 3.7 %all-to-all-start.7 = ((f32[8,320,32]{1,2,0:T(8,128)}), f32[8,320,32]{1,2,0:T(8,128)S(1)}, u32[]{:S(2)}, u32[]{:S(2)}) async-start(f32[8,320,32]{1,2,0:T(8,128)} %bitcast.32), calls=%async_computation.7 | async-start | bytes 786432 | tf_op jit(solution)/shard_map/all_to_all | solution.py:40
  340.8 6.5 %all-to-all-done.7 = f32[8,320,32]{1,2,0:T(8,128)S(1)} async-done(((f32[8,320,32]{1,2,0:T(8,128)}), f32[8,320,32]{1,2,0:T(8,128)S(1)}, u32[]{:S(2)}, u32[]{:S(2)}) %all-to-all-start.7) | async-done | bytes 327712 | tf_op jit(solution)/shard_map/all_to_all | solution.py:40
  (154 shorter events, 42.1 us)
Async XLA Ops:
  0.6 2.1 copy-start
  0.6 20.2 %copy-start.2 = (bf16[512,1024]{1,0:T(8,128)(2,1)S(1)}, bf16[512,1024]{1,0:T(8,128)(2,1)}, u32[]{:S(2)}) copy-start(bf16[512,1024]{1,0:T(8,128)(2,1)} %param.18) | copy-start | bytes 3145732
  2.7 0.6 copy-start.9
  3.2 18.9 %copy-start.5 = (bf16[1024,128]{1,0:T(8,128)(2,1)S(1)}, bf16[1024,128]{1,0:T(8,128)(2,1)}, u32[]{:S(2)}) copy-start(bf16[1024,128]{1,0:T(8,128)(2,1)} %param.19) | copy-start | bytes 786436
  4.3 30.5 %all-to-all-start.4 = ((f32[32,1,512]{2,1,0:T(1,128)}), f32[32,1,512]{2,1,0:T(1,128)S(1)}, u32[]{:S(2)}, u32[]{:S(2)}) async-start(f32[32,1,512]{2,1,0:T(1,128)} %reshape.280), calls=%async_computation.4 | async-start | bytes 131072 | tf_op jit(solution)/shard_map/all_to_all | solution.py:24
  34.6 1.2 copy-start.13
  34.6 1.2 copy-start.15
  34.7 15.9 %copy-start.3 = (bf16[1032,1,128]{2,0,1:T(8,128)(2,1)}, bf16[1032,1,128]{2,0,1:T(8,128)(2,1)S(1)}, u32[]{:S(2)}) copy-start(bf16[1032,1,128]{2,0,1:T(8,128)(2,1)S(1)} %get-tuple-element.355) | copy-start | bytes 792580
  34.7 14.5 %copy-start.19 = (bf16[4,16,128]{2,1,0:T(8,128)(2,1)S(1)}, bf16[4,16,128]{2,1,0:T(8,128)(2,1)}, u32[]{:S(2)}) copy-start(bf16[4,16,128]{2,1,0:T(8,128)(2,1)} %param.27) | copy-start | bytes 49156
  34.7 16.0 %copy-start.6 = (bf16[1024,128]{1,0:T(8,128)(2,1)S(1)}, bf16[1024,128]{1,0:T(8,128)(2,1)}, u32[]{:S(2)}) copy-start(bf16[1024,128]{1,0:T(8,128)(2,1)} %param.20) | copy-start | bytes 786436
  34.7 16.0 %copy-start.11 = (bf16[8,128]{1,0:T(8,128)(2,1)S(1)}, bf16[8,128]{1,0:T(8,128)(2,1)}, u32[]{:S(2)}) copy-start(bf16[8,128]{1,0:T(8,128)(2,1)} %param.22) | copy-start | bytes 6148
  34.7 16.5 %copy-start.17 = (pred[4,4]{1,0:T(4,128)(4,1)}, pred[4,4]{1,0:T(4,128)(4,1)S(1)}, u32[]{:S(2)}) copy-start(pred[4,4]{1,0:T(4,128)(4,1)S(1)} %iota_compare_fusion.3) | copy-start | bytes 52
  34.7 1.1 copy-start.7
  35.9 43.1 %all-to-all-start = ((f32[64,8,512]{2,1,0:T(8,128)}), f32[64,8,512]{2,1,0:T(8,128)S(1)}, u32[]{:S(2)}, u32[]{:S(2)}) async-start(f32[64,8,512]{2,1,0:T(8,128)} %broadcast_in_dim.119), calls=%async_computation | async-start | bytes 2097152 | tf_op jit(solution)/shard_map/all_to_all | solution.py:24
  54.2 24.9 %copy-start.4 = (bf16[1032,1,128]{2,0,1:T(8,128)(2,1)S(1)}, bf16[1032,1,128]{2,0,1:T(8,128)(2,1)}, u32[]{:S(2)}) copy-start(bf16[1032,1,128]{2,0,1:T(8,128)(2,1)} %copy-done.3) | copy-start | bytes 792580
  54.2 24.9 %copy-start.14 = (s32[1032]{0:T(1024)S(1)}, s32[1032]{0:T(1024)}, u32[]{:S(2)}) copy-start(s32[1032]{0:T(1024)} %copy-done.13) | copy-start | bytes 12388
  54.2 24.9 %copy-start.16 = (s32[512]{0:T(512)S(1)}, s32[512]{0:T(512)}, u32[]{:S(2)}) copy-start(s32[512]{0:T(512)} %copy-done.15) | copy-start | bytes 6148
  116.5 19.7 %all-to-all-start.5 = ((f32[32,1,2064]{2,1,0:T(1,128)}), f32[32,1,2064]{2,1,0:T(1,128)S(1)}, u32[]{:S(2)}, u32[]{:S(2)}) async-start(f32[32,1,2064]{2,1,0:T(1,128)} %all_to_all.33), calls=%async_computation.5 | async-start | bytes 557056 | tf_op jit(solution)/shard_map/all_to_all | solution.py:40
  136.2 73.0 %all-to-all-start.2 = ((f32[32,8,8,129]{3,2,1,0:T(8,128)}), f32[32,8,8,129]{3,2,1,0:T(8,128)S(1)}, u32[]{:S(2)}, u32[]{:S(2)}) async-start(f32[32,8,8,129]{3,2,1,0:T(8,128)} %copy.196), calls=%async_computation.2 | async-start | bytes 4194304 | tf_op jit(solution)/shard_map/all_to_all | solution.py:47
  210.1 28.3 %copy-start.10 = (bf16[8,128]{1,0:T(8,128)(2,1)S(1)}, bf16[8,128]{1,0:T(8,128)(2,1)}, u32[]{:S(2)}) copy-start(bf16[8,128]{1,0:T(8,128)(2,1)} %param.21) | copy-start | bytes 6148
  210.1 28.3 %copy-start.12 = (bf16[8,128]{1,0:T(8,128)(2,1)S(1)}, bf16[8,128]{1,0:T(8,128)(2,1)}, u32[]{:S(2)}) copy-start(bf16[8,128]{1,0:T(8,128)(2,1)} %param.22) | copy-start | bytes 6148
  210.1 21.0 %all-to-all-start.6 = ((f32[32,1,2064]{2,1,0:T(1,128)}), f32[32,1,2064]{2,1,0:T(1,128)S(1)}, u32[]{:S(2)}, u32[]{:S(2)}) async-start(f32[32,1,2064]{2,1,0:T(1,128)} %broadcast_in_dim.130), calls=%async_computation.6 | async-start | bytes 557056 | tf_op jit(solution)/shard_map/all_to_all | solution.py:24
  218.9 107.5 %copy-start.18 = (pred[4,4]{1,0:T(4,128)(4,1)S(1)}, pred[4,4]{1,0:T(4,128)(4,1)}, u32[]{:S(2)}) copy-start(pred[4,4]{1,0:T(4,128)(4,1)} %copy-done.17) | copy-start | bytes 52
  219.0 107.3 %copy-start.8 = (f32[16,1,8,4,4]{2,4,3,0,1:T(4,128)S(1)}, f32[16,1,8,4,4]{2,4,3,0,1:T(4,128)}, u32[]{:S(2)}) copy-start(f32[16,1,8,4,4]{2,4,3,0,1:T(4,128)} %get-tuple-element.188) | copy-start | bytes 24580
  232.1 101.5 %all-to-all-start.3 = ((bf16[32,8,8,128]{3,2,1,0:T(8,128)(2,1)}), bf16[32,8,8,128]{3,2,1,0:T(8,128)(2,1)S(1)}, u32[]{:S(2)}, u32[]{:S(2)}) async-start(bf16[32,8,8,128]{3,2,1,0:T(8,128)(2,1)} %broadcast_in_dim.120), calls=%async_computation.3 | async-start | bytes 1048576 | tf_op jit(solution)/shard_map/all_to_all | solution.py:24
  327.2 5.8 %copy-start.20 = (bf16[4,16,128]{2,1,0:T(8,128)(2,1)S(1)}, bf16[4,16,128]{2,1,0:T(8,128)(2,1)}, u32[]{:S(2)}) copy-start(bf16[4,16,128]{2,1,0:T(8,128)(2,1)} %param.28) | copy-start | bytes 49156
  331.7 1.6 copy-start.1
  333.7 5.3 %copy-start.21 = (s32[128,1]{0,1:T(1,128)S(1)}, s32[128,1]{0,1:T(1,128)}, u32[]{:S(2)}) copy-start(s32[128,1]{0,1:T(1,128)} %param.31) | copy-start | bytes 1540
  335.2 12.1 %all-to-all-start.7 = ((f32[8,320,32]{1,2,0:T(8,128)}), f32[8,320,32]{1,2,0:T(8,128)S(1)}, u32[]{:S(2)}, u32[]{:S(2)}) async-start(f32[8,320,32]{1,2,0:T(8,128)} %bitcast.32), calls=%async_computation.7 | async-start | bytes 786432 | tf_op jit(solution)/shard_map/all_to_all | solution.py:40
where the time goes:
time: 350 us; the launch traced here: 349 us
  waiting for transfers between devices  115 us (33%)
  blocking collectives  96.6 us (28%)
  starting transfers between devices  61.8 us (18%)
  matrix products  39.1 us (11%)
  local copies, waits for them, and re-layouts  23.3 us (7%)
  other arithmetic  10.8 us (3%)
    all_gather x1, blocking collectives, in_one_piece(): result, at, done = (lax.all_gather(both, axis, axis=dim, tiled=True), 0, [])  87.8 us
    all_to_all x1, waiting for transfers between devices, sum_in_two_steps(): return jnp.sum(lax.all_to_all(own, far, 0, 0, tiled=True), axis=0)  66.6 us
    all_to_all x4, starting transfers between devices, from_everyone(): lax.all_to_all(jnp.broadcast_to(shard[None], (peers, *shard.shape)), axis...  44.9 us
    all_to_all x4, waiting for transfers between devices, from_everyone(): lax.all_to_all(jnp.broadcast_to(shard[None], (peers, *shard.shape)), axis...  33.8 us
    dot_general x16, matrix products, prefill_scores(): jnp.einsum('qd,kd->qk', query_rows, keys_one, preferred_element_type=jnp....  24.8 us
    all_to_all x2, waiting for transfers between devices, summed_on_arrival(): lax.all_to_all(pieces, axis, split_axis=0, concat_axis=0, tiled=True)  14.8 us
    all_to_all x2, starting transfers between devices, summed_on_arrival(): lax.all_to_all(pieces, axis, split_axis=0, concat_axis=0, tiled=True)  10.6 us
    dot_general x8, matrix products, head_sums(): jnp.dot(weights.astype(jnp.bfloat16), values_one, preferred_element_type=...  9.83 us
  transfers between devices with their start and end apart: 7, of which 5 were waited for; matrix products, arithmetic and copies ran while one was open for 10% of the time, Pallas kernels for 0%

commit v1 on v0

v1 whole, which is shorter than its diff:
```python
import functools
import math

import jax
import jax.numpy as jnp
from jax import lax
from jax.experimental import pallas as pl
from jax.experimental.pallas import tpu as pltpu
from jax.sharding import Mesh
from jax.sharding import PartitionSpec as P

HEADS = 64
KV_HEADS = 8
HEAD = 128
SPAN = 512
BLOCK = 4
STEPS = 4
SEQ = ("seq_0", "seq_1")
SEQ_GROUP = ("seq_0", "seq_1", "group")
SEQ_TENSOR = ("seq_0", "seq_1", "tensor")

PEERS = 32
LOCAL = 8
ROWS = 16
SLOTS = 256
CACHED = 1024
HALF = 256
KEYS = 2 * CACHED + 128
STAT = LOCAL * HEAD
DEC = STAT + HEAD
WIDE = DEC + 2 * HEAD
THIN = STAT + 2 * HEAD
DEC_LANE = 32

NEG = -1e30
LOG2 = HEAD**-0.5 * math.log2(math.e)
bf16 = jnp.bfloat16
f32 = jnp.float32


def log_total(peak, total):
    safe = jnp.where(total > 0.0, total, 1.0)
    return jnp.where(total > 0.0, peak * LOG2 + jnp.log2(safe), NEG)


def terms(x):
    first = x.astype(bf16).astype(f32)
    rest = x - first
    second = rest.astype(bf16).astype(f32)
    return (first, second, rest - second)


def dot_t(a, b):
    return lax.dot_general(a, b, (((1,), (1,)), ((), ())), preferred_element_type=f32)


def dot(a, b):
    return lax.dot_general(a, b, (((1,), (0,)), ((), ())), preferred_element_type=f32)


def decode_kernel(place, lengths, requests, q_ref, k_ref, v_ref, nk_ref, nv_ref, out_ref, qs, os, ls, nks, nvs):
    lines = LOCAL * STEPS
    for h in range(LOCAL):
        for t in range(STEPS):
            at = (h * STEPS + t) * ROWS
            qs[at : at + ROWS, :] = q_ref[t, :, h * HEAD : (h + 1) * HEAD].astype(f32)
    for u in range(STEPS):
        nks[u * ROWS : (u + 1) * ROWS, :] = nk_ref[u].astype(f32)
        nvs[u * ROWS : (u + 1) * ROWS, :] = nv_ref[u].astype(f32)
    nks[STEPS * ROWS :, :] = jnp.zeros((STEPS * ROWS, HEAD), f32)
    nvs[STEPS * ROWS :, :] = jnp.zeros((STEPS * ROWS, HEAD), f32)
    seq = place[0]
    position = seq * SLOTS + lax.broadcasted_iota(jnp.int32, (lines, SLOTS), 1)
    step = lax.broadcasted_iota(jnp.int32, (lines, 8), 1)
    line_step = lax.broadcasted_iota(jnp.int32, (lines, 8), 0) % STEPS
    step_seen = (step <= line_step) & (seq == 0)
    for r in range(ROWS):
        length = lengths[requests[r]]
        q = qs[pl.ds(r, lines, stride=ROWS), :].astype(bf16)
        nk = nks[pl.ds(r, 8, stride=ROWS), :].astype(bf16)
        nv = nvs[pl.ds(r, 8, stride=ROWS), :].astype(bf16)
        s = dot_t(q, k_ref[r])
        s2 = dot_t(q, nk)
        seen = position < length
        s = jnp.where(seen, s, NEG)
        s2 = jnp.where(step_seen, s2, NEG)
        peak = jnp.maximum(jnp.max(s, axis=1, keepdims=True), jnp.max(s2, axis=1, keepdims=True))
        p = jnp.where(seen, jnp.exp2((s - peak) * LOG2), 0.0)
        p2 = jnp.where(step_seen, jnp.exp2((s2 - peak) * LOG2), 0.0)
        total = jnp.sum(p, axis=1, keepdims=True) + jnp.sum(p2, axis=1, keepdims=True)
        o = dot(p.astype(bf16), v_ref[r]) + dot(p2.astype(bf16), nv)
        o = o / jnp.where(total > 0.0, total, 1.0)
        os[pl.ds(r, lines, stride=ROWS), :] = o
        ls[pl.ds(r, lines, stride=ROWS), :] = jnp.broadcast_to(log_total(peak, total), (lines, HEAD))
    o = os[...].reshape(PEERS, 2, 8, HEAD)
    logs = ls[...].reshape(PEERS, 2, 8, HEAD)
    lane = lax.broadcasted_iota(jnp.int32, (PEERS, 8, HEAD), 2)
    stat = jnp.zeros((PEERS, 8, HEAD), f32)
    for b in range(2):
        out_ref[:, :, b * HEAD : (b + 1) * HEAD] = o[:, b].astype(bf16)
        for i, term in enumerate(terms(logs[:, b])):
            stat = jnp.where(lane == DEC_LANE + 3 * b + i, term, stat)
    out_ref[:, :, 2 * HEAD :] = stat.astype(bf16)


def prefill_kernel(place, q_ref, k_ref, v_ref, sk_ref, sv_ref, other_ref, dec_ref, out_ref, keys, values, stat):
    h = pl.program_id(0)
    seq, group = place[0], place[1]

    @pl.when(h == 0)
    def _():
        own_k, own_v = sk_ref[...].astype(f32), sv_ref[...].astype(f32)
        far = other_ref[2 * CACHED :, :].astype(f32)
        far_k, far_v = far[:8], far[8:]
        first = jnp.full((8, HEAD), group, jnp.int32) == 0
        near = jnp.concatenate([jnp.where(first, own_k, far_k), jnp.where(first, far_k, own_k)], axis=0)
        near_v = jnp.concatenate([jnp.where(first, own_v, far_v), jnp.where(first, far_v, own_v)], axis=0)
        keys[0:CACHED, :] = k_ref[...]
        keys[CACHED : 2 * CACHED, :] = other_ref[0:CACHED, :]
        values[0:CACHED, :] = v_ref[...]
        values[CACHED : 2 * CACHED, :] = other_ref[CACHED : 2 * CACHED, :]
        keys[2 * CACHED :, :] = jnp.zeros((HEAD, HEAD), bf16)
        values[2 * CACHED :, :] = jnp.zeros((HEAD, HEAD), bf16)
        keys[2 * CACHED : 2 * CACHED + 16, :] = near.astype(bf16)
        values[2 * CACHED : 2 * CACHED + 16, :] = near_v.astype(bf16)
        out_ref[:, :, DEC:] = dec_ref[:, :, 0 : 2 * HEAD]
        stat[...] = dec_ref[:, :, 2 * HEAD :].astype(f32)

    lane = lax.broadcasted_iota(jnp.int32, (PEERS // 2, 8, HEAD), 2)
    part = HALF // 2
    for b in range(2):
        rows = slice(b * part, (b + 1) * part)
        blocks = slice(b * PEERS // 2, (b + 1) * PEERS // 2)
        q = q_ref[rows, :]
        s = dot_t(q, keys[0 : 2 * CACHED, :])
        s2 = dot_t(q, keys[2 * CACHED :, :])
        index = lax.broadcasted_iota(jnp.int32, (part, HEAD), 1)
        query = group * HALF + b * part + lax.broadcasted_iota(jnp.int32, (part, HEAD), 0)
        seen = (index < 16) & (seq * 16 + index <= query)
        s2 = jnp.where(seen, s2, NEG)
        peak = jnp.maximum(jnp.max(s, axis=1, keepdims=True), jnp.max(s2, axis=1, keepdims=True))
        p = jnp.exp2((s - peak) * LOG2)
        p2 = jnp.where(seen, jnp.exp2((s2 - peak) * LOG2), 0.0)
        total = jnp.sum(p, axis=1, keepdims=True) + jnp.sum(p2, axis=1, keepdims=True)
        o = dot(p.astype(bf16), values[0 : 2 * CACHED, :]) + dot(p2.astype(bf16), values[2 * CACHED :, :])
        o = (o / total).reshape(PEERS // 2, 8, HEAD)
        out_ref[blocks, :, pl.ds(pl.multiple_of(h * HEAD, HEAD), HEAD)] = o.astype(bf16)
        logs = jnp.broadcast_to(log_total(peak, total), (part, HEAD)).reshape(PEERS // 2, 8, HEAD)
        now = stat[blocks]
        for i, term in enumerate(terms(logs)):
            now = jnp.where(lane == 3 * h + i, term, now)
        stat[blocks] = now

    @pl.when(h == LOCAL - 1)
    def _():
        out_ref[:, :, STAT:DEC] = stat[...].astype(bf16)


def combine_kernel(in_ref, out_ref):
    t = in_ref[:, :, STAT:DEC].astype(f32).reshape(PEERS * 8, HEAD)
    logs = t + pltpu.roll(t, HEAD - 1, 1) + pltpu.roll(t, HEAD - 2, 1)
    logs = logs.reshape(PEERS, 8, HEAD)
    share = jnp.exp2(logs - jnp.max(logs, axis=0)[None])
    share = share / jnp.sum(share, axis=0)[None]
    for j in range(LOCAL + 2):
        lane = 3 * j if j < LOCAL else DEC_LANE + 3 * (j - LOCAL)
        at = j * HEAD if j < LOCAL else DEC + (j - LOCAL) * HEAD
        x = in_ref[:, :, at : at + HEAD].astype(f32)
        total = jnp.sum(x * share[:, :, lane : lane + 1], axis=0)
        out_ref[:, :, j * HEAD : (j + 1) * HEAD] = jnp.broadcast_to(total[None], (PEERS, 8, HEAD)).astype(bf16)


def project_kernel(in_ref, w_ref, out_ref, rows):
    rows[0:HALF, :] = in_ref[:, :, 0:STAT].astype(f32).reshape(HALF, STAT)
    for h in range(LOCAL):
        for t in range(STEPS):
            for b in range(2):
                at = HALF + t * ROWS + b * 8
                x = in_ref[h * STEPS + t, :, STAT + b * HEAD : STAT + (b + 1) * HEAD]
                rows[at : at + 8, h * HEAD : (h + 1) * HEAD] = x.astype(f32)
    y = dot(rows[...].astype(bf16), w_ref[...])
    y = jnp.concatenate([y, jnp.zeros((HEAD // 2, y.shape[1]), f32)], axis=0)
    y = y.T
    out_ref[...] = y.reshape(8, 32, 3 * HEAD)


def last_kernel(in_ref, prefill_ref, decode_ref):
    y = jnp.sum(in_ref[...], axis=0)
    prefill_ref[...] = y[:, 0:HALF].astype(bf16)
    decode_ref[...] = y[:, HALF : HALF + HEAD].T[: STEPS * ROWS].reshape(STEPS, ROWS, 32).astype(bf16)


def landing_kernel(place, row_ref, in_ref, keys_ref, values_ref):
    owner = place[0] * 2 + place[1]
    blocks = SPAN // BLOCK
    row = row_ref[...]
    column = jnp.broadcast_to(row.astype(f32), (blocks, blocks)).T.astype(jnp.int32)
    earlier = lax.broadcasted_iota(jnp.int32, (blocks, blocks), 0) < lax.broadcasted_iota(
        jnp.int32, (blocks, blocks), 1
    )
    same = (column == row) & earlier
    rank = jnp.sum(jnp.where(same, 1.0, 0.0), axis=0, keepdims=True)
    code = jnp.broadcast_to(jnp.where(row == owner, rank, -1.0), (16, blocks)).astype(bf16)
    spread = lax.broadcasted_iota(jnp.int32, (blocks, SPAN), 1) // BLOCK
    spread = spread == lax.broadcasted_iota(jnp.int32, (blocks, SPAN), 0)
    code = dot(code, jnp.where(spread, 1.0, 0.0).astype(bf16))
    line = lax.broadcasted_iota(jnp.int32, (16, SPAN), 0)
    token = lax.broadcasted_iota(jnp.int32, (16, SPAN), 1) % BLOCK
    chosen = (code == (line // BLOCK).astype(f32)) & (token == line % BLOCK)
    x = in_ref[...].reshape(SPAN, 2 * HEAD)
    y = dot(jnp.where(chosen, 1.0, 0.0).astype(bf16), x)
    keys_ref[...] = y[:, :HEAD].astype(bf16)
    values_ref[...] = y[:, HEAD:].astype(bf16)


def cost(flops, moved, exps=0):
    return pl.CostEstimate(flops=flops, bytes_accessed=moved, transcendentals=exps)


SMEM = pl.BlockSpec(memory_space=pltpu.SMEM)
VMEM = pl.BlockSpec(memory_space=pltpu.VMEM)


def swap(x, axis):
    return lax.all_to_all(x, axis, 0, 0, tiled=True)


def body(
    prefill_queries,
    cached_keys,
    cached_values,
    span_keys,
    span_values,
    out_weight,
    decode_queries,
    decode_keys,
    decode_values,
    new_keys,
    new_values,
    request_lengths,
    row_requests,
    block_table,
):
    seq = lax.axis_index(SEQ)
    group = lax.axis_index("group")
    place = jnp.stack([seq, group]).astype(jnp.int32)
    blocks = jnp.concatenate([span_keys, span_values], axis=1)
    landed = swap(jnp.broadcast_to(blocks[None], (2 * PEERS, *blocks.shape)), SEQ_GROUP)
    mine = jnp.concatenate([cached_keys, cached_values, span_keys, span_values], axis=0)
    other = lax.ppermute(mine, "group", [(0, 1), (1, 0)])

    lines = LOCAL * STEPS * ROWS
    decoded = pl.pallas_call(
        decode_kernel,
        name="decode",
        out_shape=jax.ShapeDtypeStruct((PEERS, 8, 3 * HEAD), bf16),
        in_specs=[SMEM] * 3 + [VMEM] * 5,
        out_specs=VMEM,
        scratch_shapes=[pltpu.VMEM((lines, HEAD), f32)] * 3 + [pltpu.VMEM((2 * STEPS * ROWS, HEAD), f32)] * 2,
        cost_estimate=cost(2 * 2 * 512 * SLOTS * HEAD * 8, 3 << 20, 512 * SLOTS),
    )(place, request_lengths, row_requests, decode_queries, decode_keys, decode_values, new_keys, new_values)

    whole2 = lambda h, place: (0, 0)
    whole3 = lambda h, place: (0, 0, 0)
    packed = pl.pallas_call(
        prefill_kernel,
        name="prefill",
        out_shape=jax.ShapeDtypeStruct((PEERS, 8, WIDE), bf16),
        grid_spec=pltpu.PrefetchScalarGridSpec(
            num_scalar_prefetch=1,
            grid=(LOCAL,),
            in_specs=[
                pl.BlockSpec((HALF, HEAD), lambda h, place: (place[1], h)),
                pl.BlockSpec((CACHED, HEAD), whole2),
                pl.BlockSpec((CACHED, HEAD), whole2),
                pl.BlockSpec((8, HEAD), whole2),
                pl.BlockSpec((8, HEAD), whole2),
                pl.BlockSpec((2 * CACHED + 16, HEAD), whole2),
                pl.BlockSpec((PEERS, 8, 3 * HEAD), whole3),
            ],
            out_specs=pl.BlockSpec((PEERS, 8, WIDE), whole3),
            scratch_shapes=[
                pltpu.VMEM((KEYS, HEAD), bf16),
                pltpu.VMEM((KEYS, HEAD), bf16),
                pltpu.VMEM((PEERS, 8, HEAD), f32),
            ],
        ),
        compiler_params=pltpu.CompilerParams(dimension_semantics=("arbitrary",)),
        cost_estimate=cost(4 * HALF * LOCAL * KEYS * HEAD, 4 << 20, HALF * LOCAL * KEYS),
    )(place, prefill_queries, cached_keys, cached_values, span_keys, span_values, other, decoded)

    arrived = swap(packed, SEQ)
    arrived, landed = lax.optimization_barrier((arrived, landed))
    attention = pl.pallas_call(
        combine_kernel,
        name="combine",
        out_shape=jax.ShapeDtypeStruct((PEERS, 8, THIN), bf16),
        in_specs=[VMEM],
        out_specs=VMEM,
        cost_estimate=cost(1 << 20, 2 << 20),
    )(arrived)
    attention = swap(attention, SEQ)
    columns = out_weight.shape[1]
    partial = pl.pallas_call(
        project_kernel,
        name="project",
        out_shape=jax.ShapeDtypeStruct((8, columns // 8, 3 * HEAD), f32),
        in_specs=[VMEM] * 2,
        out_specs=VMEM,
        scratch_shapes=[pltpu.VMEM((HALF + STEPS * ROWS, STAT), f32)],
        cost_estimate=cost(2 * 320 * STAT * columns, 2 << 20),
    )(attention, out_weight)
    partial = swap(partial, "tensor")
    prefill_out, decode_out = pl.pallas_call(
        last_kernel,
        name="last",
        out_shape=(
            jax.ShapeDtypeStruct((columns // 8, HALF), bf16),
            jax.ShapeDtypeStruct((STEPS, ROWS, columns // 8), bf16),
        ),
        in_specs=[VMEM],
        out_specs=(VMEM, VMEM),
        cost_estimate=cost(1 << 18, 1 << 19),
    )(partial)
    landed_keys, landed_values = pl.pallas_call(
        landing_kernel,
        name="landing",
        out_shape=(jax.ShapeDtypeStruct((16, HEAD), bf16), jax.ShapeDtypeStruct((16, HEAD), bf16)),
        in_specs=[SMEM] + [VMEM] * 2,
        out_specs=(VMEM, VMEM),
        cost_estimate=cost(1 << 22, 1 << 19),
    )(place, block_table.reshape(1, -1), landed)
    shape = (1, 4, BLOCK, HEAD)
    return (prefill_out.T, decode_out, landed_keys.reshape(shape), landed_values.reshape(shape))


def solution(mesh):
    torus = Mesh(
        mesh.devices.reshape(4, 8, mesh.shape["tensor"], mesh.shape["group"]),
        ("seq_0", "seq_1", "tensor", "group"),
    )
    in_specs = (
        P(None, "tensor"),
        P(SEQ_GROUP, "tensor"),
        P(SEQ_GROUP, "tensor"),
        P(SEQ_GROUP, "tensor"),
        P(SEQ_GROUP, "tensor"),
        P("tensor", SEQ),
        P(None, "group", "tensor"),
        P("group", SEQ, "tensor"),
        P("group", SEQ, "tensor"),
        P(None, "group", "tensor"),
        P(None, "group", "tensor"),
        P(),
        P("group"),
        P(),
    )
    out_specs = (
        P("group", SEQ_TENSOR),
        P(None, "group", SEQ_TENSOR),
        P(SEQ_GROUP, None, None, "tensor"),
        P(SEQ_GROUP, None, None, "tensor"),
    )
    return jax.shard_map(body, mesh=torus, in_specs=in_specs, out_specs=out_specs, check_vma=False)
```

time: 350 us -> 130 us (0.37)
  the two profiles are of different devices: /device:TPU:1 before, /device:TPU:8 now
where the time goes in v1:
time: 130 us; the launch traced here: 129 us
  blocking collectives  65.2 us (50%)
  Pallas kernels  29.4 us (23%)
  starting transfers between devices  23.6 us (18%)
  waiting for transfers between devices  6.07 us (5%)
  local copies, waits for them, and re-layouts  2.28 us (2%)
  other arithmetic  1.7 us (1%)
    all_to_all x2, blocking collectives, swap(): return lax.all_to_all(x, axis, 0, 0, tiled=True)  65.2 us
    all_to_all x2, starting transfers between devices, swap(): return lax.all_to_all(x, axis, 0, 0, tiled=True)  21.6 us
    pallas_call x1, Pallas kernels, body(): pl.pallas_call(prefill_kernel, name='prefill', out_shape=jax.ShapeDtypeSt...  14 us
    pallas_call x1, Pallas kernels, body(): pl.pallas_call(decode_kernel, name='decode', out_shape=jax.ShapeDtypeStru...  6.84 us
    all_to_all x2, waiting for transfers between devices, swap(): return lax.all_to_all(x, axis, 0, 0, tiled=True)  6.07 us
  transfers between devices with their start and end apart: 3, of which 1 were waited for; matrix products, arithmetic and copies ran while one was open for 1% of the time, Pallas kernels for 18%

profile of v1, /device:TPU:8, one launch (start us, length us, event | category | flops | bytes accessed | tf_op | source)
XLA Modules:
  0.0 128.9 jit_solution(731378875166034067)
XLA Ops:
  0.6 0.0 copy-start.2
  0.6 0.0 copy-start.3
  0.7 1.1 pad_maximum_fusion
  1.8 1.9 %collective-permute-start = (bf16[2064,128]{1,0:T(8,128)(2,1)S(1)}, bf16[2064,128]{1,0:T(8,128)(2,1)S(1)}, u32[]{:S(2)}, u32[]{:S(2)}) collective-permute-start(bf16[2064,128]{1,0:T(8,128)(2,1)S(1)} %pad_maximum_fusion), channel_id=1, source_target_pairs={{0,1},{1,0},{2,3},{3,2},{4,5},{5,4},{6,7},{7,6},{8,9},{9,8},{10,11... | collective-permute-start | bytes 1585160 | tf_op jit(solution)/shard_map/ppermute | solution.py:250
  3.7 0.0 copy-done.2
  3.7 0.0 copy-done.3
  3.7 0.7 broadcast_in_dim.2
  4.4 16.7 %all-to-all-start.1 = ((bf16[64,8,256]{2,1,0:T(8,128)(2,1)}), bf16[64,8,256]{2,1,0:T(8,128)(2,1)S(1)}, u32[]{:S(2)}, u32[]{:S(2)}) async-start(bf16[64,8,256]{2,1,0:T(8,128)(2,1)} %broadcast_in_dim.2), calls=%async_computation.1 | async-start | bytes 524288 | tf_op jit(solution)/shard_map/all_to_all | solution.py:225
  21.1 0.6 pad_add_fusion.place
  21.7 6.8 %decode.1.dec_ref = bf16[32,8,384]{2,1,0:T(8,128)(2,1)} custom-call(s32[2]{0:T(128)} %pad_add_fusion.place, s32[32]{0:T(128)} %lengths.1, s32[16]{0:T(128)} %requests.1, bf16[4,16,1024]{2,1,0:T(8,128)(2,1)} %q_ref.2, bf16[16,256,128]{2,1,0:T(8,128)(2,1)} %k_ref.2, bf16[16,256,128]{2,1,0:T(8,128)(2,1)} %v_ref.2, bf16[4,16,128]{2,1,0:T(8,128)(2,1)} %nk_ref.1, ...), custom_call_target="tpu_custom_call" | custom-call | flops 536870912 | bytes 3145728 | tf_op jit(solution)/shard_map/decode/pallas_call | solution.py:253
  28.6 0.0 collective-permute-done.other_ref
  28.6 0.0 copy-start.4
  28.6 0.8 copy-done.4
  29.4 14.0 %prefill.1 = bf16[32,8,1408]{2,1,0:T(8,128)(2,1)} custom-call(s32[2]{0:T(128)} %pad_add_fusion.place, bf16[512,1024]{1,0:T(8,128)(2,1)} %q_ref.3, bf16[1024,128]{1,0:T(8,128)(2,1)} %k_ref.3, bf16[1024,128]{1,0:T(8,128)(2,1)} %v_ref.3, bf16[8,128]{1,0:T(8,128)(2,1)} %sk_ref.1, bf16[8,128]{1,0:T(8,128)(2,1)} %sv_ref.1, bf16[2064,128]{1,0:T(8,128)(2,1)} %copy-done.4, ...), custom_call_target="tpu_custom_call" | custom-call | flops 2281701376 | bytes 4194304 | tf_op jit(solution)/shard_map/prefill/pallas_call | solution.py:265
  43.3 0.0 all-to-all-done.1.in_ref
  43.3 0.0 copy-start.1
  43.3 37.0 %all_to_all.20.in_ref = bf16[32,8,1408]{2,1,0:T(8,128)(2,1)} all-to-all(bf16[32,8,1408]{2,1,0:T(8,128)(2,1)} %prefill.1), channel_id=1, replica_groups=mesh['seq_0'=4,'seq_1'=8,'tensor'=8,'group'=2] {'seq_0','seq_1'}, dimensions={0} | all-to-all | bytes 1441792 | tf_op jit(solution)/shard_map/all_to_all | solution.py:225
  80.3 2.5 %combine.1 = bf16[32,8,1280]{2,1,0:T(8,128)(2,1)} custom-call(bf16[32,8,1408]{2,1,0:T(8,128)(2,1)} %all_to_all.20.in_ref), custom_call_target="tpu_custom_call" | custom-call | flops 1048576 | bytes 2097152 | tf_op jit(solution)/shard_map/combine/pallas_call | solution.py:294
  82.8 0.0 copy-done.1
  82.8 28.3 %all_to_all.21.in_ref = bf16[32,8,1280]{2,1,0:T(8,128)(2,1)} all-to-all(bf16[32,8,1280]{2,1,0:T(8,128)(2,1)} %combine.1), channel_id=1, replica_groups=mesh['seq_0'=4,'seq_1'=8,'tensor'=8,'group'=2] {'seq_0','seq_1'}, dimensions={0} | all-to-all | bytes 1310720 | tf_op jit(solution)/shard_map/all_to_all | solution.py:225
  111.1 2.4 %project.1 = f32[8,32,384]{2,1,0:T(8,128)} custom-call(bf16[32,8,1280]{2,1,0:T(8,128)(2,1)} %all_to_all.21.in_ref, bf16[1024,256]{1,0:T(8,128)(2,1)} %w_ref.1), custom_call_target="tpu_custom_call" | custom-call | flops 167772160 | bytes 2097152 | tf_op jit(solution)/shard_map/project/pallas_call | solution.py:304
  113.5 5.0 %all-to-all-start.3 = ((f32[8,32,384]{2,1,0:T(8,128)}), f32[8,32,384]{2,1,0:T(8,128)S(1)}, u32[]{:S(2)}, u32[]{:S(2)}) async-start(f32[8,32,384]{2,1,0:T(8,128)} %project.1), calls=%async_computation.3 | async-start | bytes 786432 | tf_op jit(solution)/shard_map/all_to_all | solution.py:225
  118.5 1.9 %landing.1 = (bf16[16,128]{1,0:T(8,128)(2,1)}, bf16[16,128]{1,0:T(8,128)(2,1)}) custom-call(s32[2]{0:T(128)} %pad_add_fusion.place, s32[1,128]{1,0:T(1,128)} %bitcast.6, bf16[64,8,256]{2,1,0:T(8,128)(2,1)} %copy-done.1), custom_call_target="tpu_custom_call" | custom-call | flops 4194304 | bytes 524288 | tf_op jit(solution)/shard_map/landing/pallas_call | solution.py:325
  120.4 6.1 %all-to-all-done.3.in_ref = f32[8,32,384]{2,1,0:T(8,128)S(1)} async-done(((f32[8,32,384]{2,1,0:T(8,128)}), f32[8,32,384]{2,1,0:T(8,128)S(1)}, u32[]{:S(2)}, u32[]{:S(2)}) %all-to-all-start.3) | async-done | bytes 393248 | tf_op jit(solution)/shard_map/all_to_all | solution.py:225
  126.5 0.0 copy-start
  126.5 0.7 copy-done
  127.2 1.7 %last.1 = (bf16[32,256]{1,0:T(8,128)(2,1)}, bf16[4,16,32]{2,1,0:T(8,128)(2,1)}) custom-call(f32[8,32,384]{2,1,0:T(8,128)} %copy-done), custom_call_target="tpu_custom_call" | custom-call | flops 262144 | bytes 524288 | tf_op jit(solution)/shard_map/last/pallas_call | solution.py:314
  (1 shorter events, 0.0 us)
Async XLA Ops:
  0.6 3.1 %copy-start.2 = (bf16[8,128]{1,0:T(8,128)(2,1)S(1)}, bf16[8,128]{1,0:T(8,128)(2,1)}, u32[]{:S(2)}) copy-start(bf16[8,128]{1,0:T(8,128)(2,1)} %sk_ref.1) | copy-start | bytes 6148
  0.6 3.1 %copy-start.3 = (bf16[8,128]{1,0:T(8,128)(2,1)S(1)}, bf16[8,128]{1,0:T(8,128)(2,1)}, u32[]{:S(2)}) copy-start(bf16[8,128]{1,0:T(8,128)(2,1)} %sv_ref.1) | copy-start | bytes 6148
  1.8 26.8 %collective-permute-start = (bf16[2064,128]{1,0:T(8,128)(2,1)S(1)}, bf16[2064,128]{1,0:T(8,128)(2,1)S(1)}, u32[]{:S(2)}, u32[]{:S(2)}) collective-permute-start(bf16[2064,128]{1,0:T(8,128)(2,1)S(1)} %pad_maximum_fusion), channel_id=1, source_target_pairs={{0,1},{1,0},{2,3},{3,2},{4,5},{5,4},{6,7},{7,6},{8,9},{9,8},{10,11... | collective-permute-start | bytes 1585160 | tf_op jit(solution)/shard_map/ppermute | solution.py:250
  4.4 38.9 %all-to-all-start.1 = ((bf16[64,8,256]{2,1,0:T(8,128)(2,1)}), bf16[64,8,256]{2,1,0:T(8,128)(2,1)S(1)}, u32[]{:S(2)}, u32[]{:S(2)}) async-start(bf16[64,8,256]{2,1,0:T(8,128)(2,1)} %broadcast_in_dim.2), calls=%async_computation.1 | async-start | bytes 524288 | tf_op jit(solution)/shard_map/all_to_all | solution.py:225
  28.6 0.8 copy-start.4
  43.3 39.5 %copy-start.1 = (bf16[64,8,256]{2,1,0:T(8,128)(2,1)}, bf16[64,8,256]{2,1,0:T(8,128)(2,1)S(1)}, u32[]{:S(2)}) copy-start(bf16[64,8,256]{2,1,0:T(8,128)(2,1)S(1)} %all-to-all-done.1.in_ref) | copy-start | bytes 786436
  113.5 13.0 %all-to-all-start.3 = ((f32[8,32,384]{2,1,0:T(8,128)}), f32[8,32,384]{2,1,0:T(8,128)S(1)}, u32[]{:S(2)}, u32[]{:S(2)}) async-start(f32[8,32,384]{2,1,0:T(8,128)} %project.1), calls=%async_computation.3 | async-start | bytes 786432 | tf_op jit(solution)/shard_map/all_to_all | solution.py:225
  126.5 0.7 copy-start

commit v2 on v1

v2 whole, which is shorter than its diff:
```python
import functools
import math

import jax
import jax.numpy as jnp
from jax import lax
from jax.experimental import pallas as pl
from jax.experimental.pallas import tpu as pltpu
from jax.sharding import Mesh
from jax.sharding import PartitionSpec as P

HEADS = 64
KV_HEADS = 8
HEAD = 128
SPAN = 512
BLOCK = 4
STEPS = 4
SEQ = ("seq_0", "seq_1")
SEQ_GROUP = ("seq_0", "seq_1", "group")
SEQ_TENSOR = ("seq_0", "seq_1", "tensor")

PEERS = 32
LOCAL = 8
ROWS = 16
SLOTS = 256
CACHED = 1024
HALF = 256
KEYS = 2 * CACHED + 128
STAT = LOCAL * HEAD
DEC = STAT + HEAD
NEW = DEC + 2 * HEAD
WIDE = NEW + 2 * HEAD
THIN = STAT + 2 * HEAD
DEC_LANE = 32

NEG = -1e30
LOG2 = HEAD**-0.5 * math.log2(math.e)
bf16 = jnp.bfloat16
f32 = jnp.float32


def log_total(peak, total):
    safe = jnp.where(total > 0.0, total, 1.0)
    return jnp.where(total > 0.0, peak * LOG2 + jnp.log2(safe), NEG)


def terms(x):
    first = x.astype(bf16).astype(f32)
    rest = x - first
    second = rest.astype(bf16).astype(f32)
    return (first, second, rest - second)


def dot_t(a, b):
    return lax.dot_general(a, b, (((1,), (1,)), ((), ())), preferred_element_type=f32)


def dot(a, b):
    return lax.dot_general(a, b, (((1,), (0,)), ((), ())), preferred_element_type=f32)


def decode_kernel(lengths, requests, q_ref, k_ref, v_ref, nk_ref, nv_ref, out_ref, qs, os, ls, nks, nvs):
    lines = LOCAL * STEPS
    for h in range(LOCAL):
        for t in range(STEPS):
            at = (h * STEPS + t) * ROWS
            qs[at : at + ROWS, :] = q_ref[t, :, h * HEAD : (h + 1) * HEAD].astype(f32)
    for u in range(STEPS):
        nks[u * ROWS : (u + 1) * ROWS, :] = nk_ref[u].astype(f32)
        nvs[u * ROWS : (u + 1) * ROWS, :] = nv_ref[u].astype(f32)
    nks[STEPS * ROWS :, :] = jnp.zeros((STEPS * ROWS, HEAD), f32)
    nvs[STEPS * ROWS :, :] = jnp.zeros((STEPS * ROWS, HEAD), f32)
    seq = lax.axis_index(SEQ)
    position = seq * SLOTS + lax.broadcasted_iota(jnp.int32, (lines, SLOTS), 1)
    step = lax.broadcasted_iota(jnp.int32, (ROWS * lines, 8), 1)
    line_step = lax.broadcasted_iota(jnp.int32, (ROWS * lines, 8), 0) % STEPS
    step_seen = (step <= line_step) & (seq == 0)
    scores, step_scores, step_values = [], [], []
    for r in range(ROWS):
        q = qs[pl.ds(r, lines, stride=ROWS), :].astype(bf16)
        nk = nks[pl.ds(r, 8, stride=ROWS), :].astype(bf16)
        step_values.append(nvs[pl.ds(r, 8, stride=ROWS), :].astype(bf16))
        scores.append(jnp.where(position < lengths[requests[r]], dot_t(q, k_ref[r]), NEG))
        step_scores.append(dot_t(q, nk))
    s = jnp.concatenate(scores, axis=0)
    s2 = jnp.where(step_seen, jnp.concatenate(step_scores, axis=0), NEG)
    peak = jnp.maximum(jnp.max(s, axis=1, keepdims=True), jnp.max(s2, axis=1, keepdims=True))
    p = jnp.where(s > 0.5 * NEG, jnp.exp2((s - peak) * LOG2), 0.0)
    p2 = jnp.where(step_seen, jnp.exp2((s2 - peak) * LOG2), 0.0)
    total = jnp.sum(p, axis=1, keepdims=True) + jnp.sum(p2, axis=1, keepdims=True)
    p, p2 = p.astype(bf16), p2.astype(bf16)
    inverse = 1.0 / jnp.where(total > 0.0, total, 1.0)
    logs = log_total(peak, total)
    for r in range(ROWS):
        at = slice(r * lines, (r + 1) * lines)
        o = dot(p[at], v_ref[r]) + dot(p2[at], step_values[r])
        os[pl.ds(r, lines, stride=ROWS), :] = o * inverse[at]
        ls[pl.ds(r, lines, stride=ROWS), :] = jnp.broadcast_to(logs[at], (lines, HEAD))
    o = os[...].reshape(PEERS, 2, 8, HEAD)
    logs = ls[...].reshape(PEERS, 2, 8, HEAD)
    lane = lax.broadcasted_iota(jnp.int32, (PEERS, 8, HEAD), 2)
    stat = jnp.zeros((PEERS, 8, HEAD), f32)
    for b in range(2):
        out_ref[:, :, b * HEAD : (b + 1) * HEAD] = o[:, b].astype(bf16)
        for i, term in enumerate(terms(logs[:, b])):
            stat = jnp.where(lane == DEC_LANE + 3 * b + i, term, stat)
    out_ref[:, :, 2 * HEAD :] = stat.astype(bf16)


def prefill_kernel(q_ref, k_ref, v_ref, sk_ref, sv_ref, other_ref, dec_ref, out_ref, keys, values):
    seq, group = lax.axis_index(SEQ), lax.axis_index("group")
    own_k, own_v = sk_ref[...].astype(f32), sv_ref[...].astype(f32)
    far = other_ref[2 * CACHED :, :].astype(f32)
    far_k, far_v = far[:8], far[8:]
    first = jnp.full((8, HEAD), group, jnp.int32) == 0
    near_k = jnp.concatenate([jnp.where(first, own_k, far_k), jnp.where(first, far_k, own_k)], axis=0)
    near_v = jnp.concatenate([jnp.where(first, own_v, far_v), jnp.where(first, far_v, own_v)], axis=0)
    keys[0:CACHED, :] = k_ref[...]
    keys[CACHED : 2 * CACHED, :] = other_ref[0:CACHED, :]
    values[0:CACHED, :] = v_ref[...]
    values[CACHED : 2 * CACHED, :] = other_ref[CACHED : 2 * CACHED, :]
    keys[2 * CACHED :, :] = jnp.zeros((HEAD, HEAD), bf16)
    values[2 * CACHED :, :] = jnp.zeros((HEAD, HEAD), bf16)
    keys[2 * CACHED : 2 * CACHED + 16, :] = near_k.astype(bf16)
    values[2 * CACHED : 2 * CACHED + 16, :] = near_v.astype(bf16)
    out_ref[:, :, DEC:NEW] = dec_ref[:, :, 0 : 2 * HEAD]
    out_ref[:, :, NEW : NEW + HEAD] = jnp.broadcast_to(own_k[None], (PEERS, 8, HEAD)).astype(bf16)
    out_ref[:, :, NEW + HEAD :] = jnp.broadcast_to(own_v[None], (PEERS, 8, HEAD)).astype(bf16)

    lane = lax.broadcasted_iota(jnp.int32, (PEERS, 8, HEAD), 2)
    index = lax.broadcasted_iota(jnp.int32, (HALF, HEAD), 1)
    query = group * HALF + lax.broadcasted_iota(jnp.int32, (HALF, HEAD), 0)
    seen = (index < 16) & (seq * 16 + index <= query)
    mine = pl.ds(pl.multiple_of(group * HALF, HALF), HALF)

    def scores(h):
        s = dot_t(q_ref[mine, h * HEAD : (h + 1) * HEAD], keys[...])
        return jnp.concatenate([s[:, : 2 * CACHED], jnp.where(seen, s[:, 2 * CACHED :], NEG)], axis=1)

    upcoming = scores(0)
    stat = dec_ref[:, :, 2 * HEAD :].astype(f32)
    for h in range(LOCAL):
        s = upcoming
        if h + 1 < LOCAL:
            upcoming = scores(h + 1)
        peak = jnp.max(s, axis=1, keepdims=True)
        edge = s[:, 2 * CACHED :]
        p = jnp.exp2((s[:, : 2 * CACHED] - peak) * LOG2)
        p = jnp.concatenate([p, jnp.where(seen, jnp.exp2((edge - peak) * LOG2), 0.0)], axis=1)
        total = jnp.sum(p, axis=1, keepdims=True)
        o = dot(p.astype(bf16), values[...])
        o = (o / total).reshape(PEERS, 8, HEAD)
        out_ref[:, :, h * HEAD : (h + 1) * HEAD] = o.astype(bf16)
        logs = jnp.broadcast_to(log_total(peak, total), (HALF, HEAD)).reshape(PEERS, 8, HEAD)
        for i, term in enumerate(terms(logs)):
            stat = jnp.where(lane == 3 * h + i, term, stat)
    out_ref[:, :, STAT:DEC] = stat.astype(bf16)


def combine_kernel(in_ref, out_ref, new_ref):
    new_ref[...] = in_ref[:, :, NEW:]
    t = in_ref[:, :, STAT:DEC].astype(f32).reshape(PEERS * 8, HEAD)
    logs = t + pltpu.roll(t, HEAD - 1, 1) + pltpu.roll(t, HEAD - 2, 1)
    logs = logs.reshape(PEERS, 8, HEAD)
    share = jnp.exp2(logs - jnp.max(logs, axis=0)[None])
    share = share / jnp.sum(share, axis=0)[None]
    for j in range(LOCAL + 2):
        lane = 3 * j if j < LOCAL else DEC_LANE + 3 * (j - LOCAL)
        at = j * HEAD if j < LOCAL else DEC + (j - LOCAL) * HEAD
        x = in_ref[:, :, at : at + HEAD].astype(f32)
        total = jnp.sum(x * share[:, :, lane : lane + 1], axis=0)
        out_ref[:, :, j * HEAD : (j + 1) * HEAD] = jnp.broadcast_to(total[None], (PEERS, 8, HEAD)).astype(bf16)


def project_kernel(in_ref, w_ref, out_ref, rows):
    rows[0:HALF, :] = in_ref[:, :, 0:STAT].astype(f32).reshape(HALF, STAT)
    for h in range(LOCAL):
        for t in range(STEPS):
            for b in range(2):
                at = HALF + t * ROWS + b * 8
                x = in_ref[h * STEPS + t, :, STAT + b * HEAD : STAT + (b + 1) * HEAD]
                rows[at : at + 8, h * HEAD : (h + 1) * HEAD] = x.astype(f32)
    y = dot(rows[...].astype(bf16), w_ref[...])
    y = jnp.concatenate([y, jnp.zeros((HEAD // 2, y.shape[1]), f32)], axis=0)
    y = y.T
    out_ref[...] = y.reshape(8, 32, 3 * HEAD).astype(bf16)


def last_kernel(in_ref, prefill_ref, decode_ref):
    y = jnp.sum(in_ref[...].astype(f32), axis=0)
    prefill_ref[...] = y[:, 0:HALF].astype(bf16)
    decode_ref[...] = y[:, HALF : HALF + HEAD].T[: STEPS * ROWS].reshape(STEPS, ROWS, 32).astype(bf16)


def landing_kernel(row_ref, own_ref, far_ref, keys_ref, values_ref):
    group = lax.axis_index("group")
    owner = lax.axis_index(SEQ) * 2 + group
    blocks, tokens = SPAN // BLOCK, SPAN // 2
    row = row_ref[...]
    column = jnp.broadcast_to(row.astype(f32), (blocks, blocks)).T.astype(jnp.int32)
    earlier = lax.broadcasted_iota(jnp.int32, (blocks, blocks), 0) < lax.broadcasted_iota(
        jnp.int32, (blocks, blocks), 1
    )
    same = (column == row) & earlier
    rank = jnp.sum(jnp.where(same, 1.0, 0.0), axis=0, keepdims=True)
    code = jnp.broadcast_to(jnp.where(row == owner, rank, -1.0), (16, blocks)).astype(bf16)
    token = lax.broadcasted_iota(jnp.int32, (blocks, tokens), 1)
    block = lax.broadcasted_iota(jnp.int32, (blocks, tokens), 0)
    line = lax.broadcasted_iota(jnp.int32, (16, tokens), 0)
    place_in = lax.broadcasted_iota(jnp.int32, (16, tokens), 1) % BLOCK

    def picked(side, ref):
        spread = (token // 8) * 4 + side * 2 + (token % 8) // BLOCK == block
        codes = dot(code, jnp.where(spread, 1.0, 0.0).astype(bf16))
        chosen = (codes == (line // BLOCK).astype(f32)) & (place_in == line % BLOCK)
        x = ref[...].astype(f32).reshape(tokens, 2 * HEAD).astype(bf16)
        return dot(jnp.where(chosen, 1.0, 0.0).astype(bf16), x)

    y = picked(group, own_ref) + picked(1 - group, far_ref)
    keys_ref[...] = y[:, :HEAD].astype(bf16)
    values_ref[...] = y[:, HEAD:].astype(bf16)


def cost(flops, moved, exps=0):
    return pl.CostEstimate(flops=flops, bytes_accessed=moved, transcendentals=exps)


SMEM = pl.BlockSpec(memory_space=pltpu.SMEM)
VMEM = pl.BlockSpec(memory_space=pltpu.VMEM)


def near(x):
    return pltpu.with_memory_space_constraint(x, pltpu.VMEM)


def swap(x, axis):
    return lax.all_to_all(x, axis, 0, 0, tiled=True)


def body(
    prefill_queries,
    cached_keys,
    cached_values,
    span_keys,
    span_values,
    out_weight,
    decode_queries,
    decode_keys,
    decode_values,
    new_keys,
    new_values,
    request_lengths,
    row_requests,
    block_table,
):
    mine = jnp.concatenate([cached_keys, cached_values, span_keys, span_values], axis=0)
    other = lax.ppermute(mine, "group", [(0, 1), (1, 0)])

    lines = LOCAL * STEPS * ROWS
    decoded = pl.pallas_call(
        decode_kernel,
        name="decode",
        out_shape=jax.ShapeDtypeStruct((PEERS, 8, 3 * HEAD), bf16),
        in_specs=[SMEM] * 2 + [VMEM] * 5,
        out_specs=VMEM,
        scratch_shapes=[pltpu.VMEM((lines, HEAD), f32)] * 3 + [pltpu.VMEM((2 * STEPS * ROWS, HEAD), f32)] * 2,
        cost_estimate=cost(2 * 2 * 512 * SLOTS * HEAD * 8, 3 << 20, 512 * SLOTS),
    )(request_lengths, row_requests, decode_queries, decode_keys, decode_values, new_keys, new_values)

    packed = pl.pallas_call(
        prefill_kernel,
        name="prefill",
        out_shape=jax.ShapeDtypeStruct((PEERS, 8, WIDE), bf16),
        in_specs=[VMEM] * 7,
        out_specs=VMEM,
        scratch_shapes=[pltpu.VMEM((KEYS, HEAD), bf16)] * 2,
        cost_estimate=cost(4 * HALF * LOCAL * KEYS * HEAD, 4 << 20, HALF * LOCAL * KEYS),
    )(
        near(prefill_queries),
        near(cached_keys),
        near(cached_values),
        span_keys,
        span_values,
        near(other),
        decoded,
    )

    arrived = swap(packed, SEQ)
    attention, new_own = pl.pallas_call(
        combine_kernel,
        name="combine",
        out_shape=(
            jax.ShapeDtypeStruct((PEERS, 8, THIN), bf16),
            jax.ShapeDtypeStruct((PEERS, 8, 2 * HEAD), bf16),
        ),
        in_specs=[VMEM],
        out_specs=(VMEM, VMEM),
        cost_estimate=cost(1 << 20, 2 << 20),
    )(near(arrived))
    new_far = lax.ppermute(new_own, "group", [(0, 1), (1, 0)])
    attention = swap(attention, SEQ)
    landed_keys, landed_values = pl.pallas_call(
        landing_kernel,
        name="landing",
        out_shape=(jax.ShapeDtypeStruct((16, HEAD), bf16), jax.ShapeDtypeStruct((16, HEAD), bf16)),
        in_specs=[VMEM] * 3,
        out_specs=(VMEM, VMEM),
        cost_estimate=cost(1 << 22, 1 << 19),
    )(block_table.reshape(1, -1), near(new_own), near(new_far))
    attention, landed_keys, landed_values = lax.optimization_barrier((attention, landed_keys, landed_values))
    columns = out_weight.shape[1]
    partial = pl.pallas_call(
        project_kernel,
        name="project",
        out_shape=jax.ShapeDtypeStruct((8, columns // 8, 3 * HEAD), bf16),
        in_specs=[VMEM] * 2,
        out_specs=VMEM,
        scratch_shapes=[pltpu.VMEM((HALF + STEPS * ROWS, STAT), f32)],
        cost_estimate=cost(2 * 320 * STAT * columns, 2 << 20),
    )(near(attention), near(out_weight))
    partial = swap(partial, "tensor")
    prefill_out, decode_out = pl.pallas_call(
        last_kernel,
        name="last",
        out_shape=(
            jax.ShapeDtypeStruct((columns // 8, HALF), bf16),
            jax.ShapeDtypeStruct((STEPS, ROWS, columns // 8), bf16),
        ),
        in_specs=[VMEM],
        out_specs=(VMEM, VMEM),
        cost_estimate=cost(1 << 18, 1 << 19),
    )(near(partial))
    shape = (1, 4, BLOCK, HEAD)
    return (prefill_out.T, decode_out, landed_keys.reshape(shape), landed_values.reshape(shape))


def solution(mesh):
    torus = Mesh(
        mesh.devices.reshape(4, 8, mesh.shape["tensor"], mesh.shape["group"]),
        ("seq_0", "seq_1", "tensor", "group"),
    )
    in_specs = (
        P(None, "tensor"),
        P(SEQ_GROUP, "tensor"),
        P(SEQ_GROUP, "tensor"),
        P(SEQ_GROUP, "tensor"),
        P(SEQ_GROUP, "tensor"),
        P("tensor", SEQ),
        P(None, "group", "tensor"),
        P("group", SEQ, "tensor"),
        P("group", SEQ, "tensor"),
        P(None, "group", "tensor"),
        P(None, "group", "tensor"),
        P(),
        P("group"),
        P(),
    )
    out_specs = (
        P("group", SEQ_TENSOR),
        P(None, "group", SEQ_TENSOR),
        P(SEQ_GROUP, None, None, "tensor"),
        P(SEQ_GROUP, None, None, "tensor"),
    )
    return jax.shard_map(body, mesh=torus, in_specs=in_specs, out_specs=out_specs, check_vma=False)
```

time: 130 us -> 104 us (0.80)
  starting transfers between devices: 23.6 us -> 10.1 us
  waiting for transfers between devices: 6.07 us -> 19.1 us
  Pallas kernels: 29.4 us -> 16.7 us
  blocking collectives: 65.2 us -> 55.6 us
  local copies, waits for them, and re-layouts: 2.28 us -> 0.03 us
    all_to_all x2 -> x1, starting transfers between devices: 21.6 us -> 6.17 us  [swap(): return lax.all_to_all(x, axis, 0, 0, tiled=True)]
    all_to_all x2 -> x1, waiting for transfers between devices: 6.07 us -> 17.8 us  [swap(): return lax.all_to_all(x, axis, 0, 0, tiled=True)]
    all_to_all x2, blocking collectives: 65.2 us -> 55.6 us  [swap(): return lax.all_to_all(x, axis, 0, 0, tiled=True)]
    pallas_call x1, Pallas kernels: 14 us -> 8.48 us  [body(): pl.pallas_call(prefill_kernel, name='prefill', out_shape=jax.ShapeDtypeSt...]
    pallas_call x1, Pallas kernels: 6.84 us -> 3.38 us  [body(): pl.pallas_call(decode_kernel, name='decode', out_shape=jax.ShapeDtypeStru...]
    ppermute x0 -> x1, starting transfers between devices: none -> 1.92 us  [body(): new_far = lax.ppermute(new_own, 'group', [(0, 1), (1, 0)])]
    unnamed x10, local copies, waits for them, and re-layouts: 1.55 us -> 0.03 us
    ppermute x0 -> x1, waiting for transfers between devices: none -> 1.31 us  [body(): new_far = lax.ppermute(new_own, 'group', [(0, 1), (1, 0)])]
  transfers between devices with their start and end apart: 3 -> 3, of which waited for: 1 -> 2; matrix products, arithmetic and copies ran while one was open for 1% -> 0% of each run, Pallas kernels for 18% -> 5%
where the time goes in v2:
time: 104 us; the launch traced here: 103 us
  blocking collectives  55.6 us (53%)
  waiting for transfers between devices  19.1 us (18%)
  Pallas kernels  16.7 us (16%)
  starting transfers between devices  10.1 us (10%)
  other arithmetic  1.1 us (1%)
    all_to_all x2, blocking collectives, swap(): return lax.all_to_all(x, axis, 0, 0, tiled=True)  55.6 us
    all_to_all x1, waiting for transfers between devices, swap(): return lax.all_to_all(x, axis, 0, 0, tiled=True)  17.8 us
    pallas_call x1, Pallas kernels, body(): pl.pallas_call(prefill_kernel, name='prefill', out_shape=jax.ShapeDtypeSt...  8.48 us
    all_to_all x1, starting transfers between devices, swap(): return lax.all_to_all(x, axis, 0, 0, tiled=True)  6.17 us
    pallas_call x1, Pallas kernels, body(): pl.pallas_call(decode_kernel, name='decode', out_shape=jax.ShapeDtypeStru...  3.38 us
  transfers between devices with their start and end apart: 3, of which 2 were waited for; matrix products, arithmetic and copies ran while one was open for 0% of the time, Pallas kernels for 5%

profile of v2, /device:TPU:8, one launch (start us, length us, event | category | flops | bytes accessed | tf_op | source)
XLA Modules:
  0.0 103.4 jit_solution(11354112549741202943)
XLA Ops:
  0.6 1.1 %pad_maximum_fusion = bf16[2064,128]{1,0:T(8,128)(2,1)S(1)} fusion(bf16[8,128]{1,0:T(8,128)(2,1)} %sv_ref.1, bf16[8,128]{1,0:T(8,128)(2,1)} %sk_ref.1, bf16[1024,128]{1,0:T(8,128)(2,1)} %v_ref.3, bf16[1024,128]{1,0:T(8,128)(2,1)} %k_ref.3), kind=kLoop, calls=%fused_computation | loop fusion | flops 2113536 | bytes 1056768 | tf_op jit(solution)/shard_map/concatenate | solution.py:256
  1.7 0.0 copy-start.1
  1.7 0.0 copy-start.2
  1.8 0.0 copy-start.4
  1.8 2.1 %collective-permute-start = (bf16[2064,128]{1,0:T(8,128)(2,1)S(1)}, bf16[2064,128]{1,0:T(8,128)(2,1)S(1)}, u32[]{:S(2)}, u32[]{:S(2)}) collective-permute-start(bf16[2064,128]{1,0:T(8,128)(2,1)S(1)} %pad_maximum_fusion), channel_id=1, source_target_pairs={{0,1},{1,0},{2,3},{3,2},{4,5},{5,4},{6,7},{7,6},{8,9},{9,8},{10,11... | collective-permute-start | bytes 1585160 | tf_op jit(solution)/shard_map/ppermute | solution.py:257
  3.8 3.4 %decode.1.dec_ref = bf16[32,8,384]{2,1,0:T(8,128)(2,1)} custom-call(s32[32]{0:T(128)} %lengths.1, s32[16]{0:T(128)} %requests.1, bf16[4,16,1024]{2,1,0:T(8,128)(2,1)} %q_ref.2, bf16[16,256,128]{2,1,0:T(8,128)(2,1)} %k_ref.2, bf16[16,256,128]{2,1,0:T(8,128)(2,1)} %v_ref.2, bf16[4,16,128]{2,1,0:T(8,128)(2,1)} %nk_ref.1, bf16[4,16,128]{2,1,0:T(8,128)(2,1)} %nv_ref.1), custom_call_target="tpu_custom_call" | custom-call | flops 536870912 | bytes 3145728 | tf_op jit(solution)/shard_map/decode/pallas_call | solution.py:260
  7.2 0.0 collective-permute-done.other_ref
  7.2 0.0 copy-done.1
  7.2 0.0 copy-done.2
  7.2 0.0 copy-done.4
  7.2 8.5 %prefill.1 = bf16[32,8,1664]{2,1,0:T(8,128)(2,1)} custom-call(bf16[512,1024]{1,0:T(8,128)(2,1)S(1)} %copy-done.4, bf16[1024,128]{1,0:T(8,128)(2,1)S(1)} %copy-done.1, bf16[1024,128]{1,0:T(8,128)(2,1)S(1)} %copy-done.2, bf16[8,128]{1,0:T(8,128)(2,1)} %sk_ref.1, bf16[8,128]{1,0:T(8,128)(2,1)} %sv_ref.1, bf16[2064,128]{1,0:T(8,128)(2,1)S(1)} %collective-permute-done.other_ref, ...), custom_call_target="tpu_custom_call" | custom-call | flops 2281701376 | bytes 4194304 | tf_op jit(solution)/shard_map/prefill/pallas_call | solution.py:270
  15.7 43.7 %all_to_all.15.in_ref = bf16[32,8,1664]{2,1,0:T(8,128)(2,1)S(1)} all-to-all(bf16[32,8,1664]{2,1,0:T(8,128)(2,1)} %prefill.1), channel_id=1, replica_groups=mesh['seq_0'=4,'seq_1'=8,'tensor'=8,'group'=2] {'seq_0','seq_1'}, dimensions={0} | all-to-all | bytes 1703936 | tf_op jit(solution)/shard_map/all_to_all | solution.py:237
  59.4 0.0 copy-start
  59.4 1.4 %combine.1 = (bf16[32,8,1280]{2,1,0:T(8,128)(2,1)}, bf16[32,8,256]{2,1,0:T(8,128)(2,1)}) custom-call(bf16[32,8,1664]{2,1,0:T(8,128)(2,1)S(1)} %all_to_all.15.in_ref), custom_call_target="tpu_custom_call" | custom-call | flops 1048576 | bytes 2097152 | tf_op jit(solution)/shard_map/combine/pallas_call | solution.py:289
  60.8 0.0 copy-start.3
  60.8 6.2 %all-to-all-start.1 = ((bf16[32,8,1280]{2,1,0:T(8,128)(2,1)}), bf16[32,8,1280]{2,1,0:T(8,128)(2,1)S(1)}, u32[]{:S(2)}, u32[]{:S(2)}) async-start(bf16[32,8,1280]{2,1,0:T(8,128)(2,1)} %get-tuple-element.13), calls=%async_computation.1 | async-start | bytes 1310720 | tf_op jit(solution)/shard_map/all_to_all | solution.py:237
  67.0 0.0 copy-done.3
  67.0 1.9 %collective-permute-start.1 = (bf16[32,8,256]{2,1,0:T(8,128)(2,1)S(1)}, bf16[32,8,256]{2,1,0:T(8,128)(2,1)S(1)}, u32[]{:S(2)}, u32[]{:S(2)}) collective-permute-start(bf16[32,8,256]{2,1,0:T(8,128)(2,1)S(1)} %copy-done.3), channel_id=1, source_target_pairs={{0,1},{1,0},{2,3},{3,2},{4,5},{5,4},{6,7},{7,6},{8,9},{9,8},{10,11... | collective-permute-start | bytes 393224 | tf_op jit(solution)/shard_map/ppermute | solution.py:300
  68.9 1.3 %collective-permute-done.1.far_ref = bf16[32,8,256]{2,1,0:T(8,128)(2,1)S(1)} collective-permute-done((bf16[32,8,256]{2,1,0:T(8,128)(2,1)S(1)}, bf16[32,8,256]{2,1,0:T(8,128)(2,1)S(1)}, u32[]{:S(2)}, u32[]{:S(2)}) %collective-permute-start.1) | collective-permute-done | bytes 131104 | tf_op jit(solution)/shard_map/ppermute | solution.py:300
  70.3 1.6 %landing.1 = (bf16[16,128]{1,0:T(8,128)(2,1)}, bf16[16,128]{1,0:T(8,128)(2,1)}) custom-call(s32[1,128]{1,0:T(1,128)} %bitcast.4, bf16[32,8,256]{2,1,0:T(8,128)(2,1)S(1)} %copy-done.3, bf16[32,8,256]{2,1,0:T(8,128)(2,1)S(1)} %collective-permute-done.1.far_ref), custom_call_target="tpu_custom_call" | custom-call | flops 4194304 | bytes 524288 | tf_op jit(solution)/shard_map/landing/pallas_call | solution.py:302
  71.9 17.8 %all-to-all-done.1.in_ref = bf16[32,8,1280]{2,1,0:T(8,128)(2,1)S(1)} async-done(((bf16[32,8,1280]{2,1,0:T(8,128)(2,1)}), bf16[32,8,1280]{2,1,0:T(8,128)(2,1)S(1)}, u32[]{:S(2)}, u32[]{:S(2)}) %all-to-all-start.1) | async-done | bytes 655392 | tf_op jit(solution)/shard_map/all_to_all | solution.py:237
  89.7 0.0 copy-done
  89.7 1.1 %project.1 = bf16[8,32,384]{2,1,0:T(8,128)(2,1)} custom-call(bf16[32,8,1280]{2,1,0:T(8,128)(2,1)S(1)} %all-to-all-done.1.in_ref, bf16[1024,256]{1,0:T(8,128)(2,1)S(1)} %copy-done), custom_call_target="tpu_custom_call" | custom-call | flops 167772160 | bytes 2097152 | tf_op jit(solution)/shard_map/project/pallas_call | solution.py:312
  90.8 11.9 %all_to_all.16.in_ref = bf16[8,32,384]{2,1,0:T(8,128)(2,1)S(1)} all-to-all(bf16[8,32,384]{2,1,0:T(8,128)(2,1)} %project.1), channel_id=1, replica_groups=mesh['seq_0'=4,'seq_1'=8,'tensor'=8,'group'=2] {'tensor'}, dimensions={0} | all-to-all | bytes 393216 | tf_op jit(solution)/shard_map/all_to_all | solution.py:237
  102.7 0.7 last.1
Async XLA Ops:
  1.7 5.5 %copy-start.1 = (bf16[1024,128]{1,0:T(8,128)(2,1)S(1)}, bf16[1024,128]{1,0:T(8,128)(2,1)}, u32[]{:S(2)}) copy-start(bf16[1024,128]{1,0:T(8,128)(2,1)} %k_ref.3) | copy-start | bytes 786436
  1.7 5.5 %copy-start.2 = (bf16[1024,128]{1,0:T(8,128)(2,1)S(1)}, bf16[1024,128]{1,0:T(8,128)(2,1)}, u32[]{:S(2)}) copy-start(bf16[1024,128]{1,0:T(8,128)(2,1)} %v_ref.3) | copy-start | bytes 786436
  1.8 5.5 %copy-start.4 = (bf16[512,1024]{1,0:T(8,128)(2,1)S(1)}, bf16[512,1024]{1,0:T(8,128)(2,1)}, u32[]{:S(2)}) copy-start(bf16[512,1024]{1,0:T(8,128)(2,1)} %q_ref.3) | copy-start | bytes 3145732
  1.8 5.4 %collective-permute-start = (bf16[2064,128]{1,0:T(8,128)(2,1)S(1)}, bf16[2064,128]{1,0:T(8,128)(2,1)S(1)}, u32[]{:S(2)}, u32[]{:S(2)}) collective-permute-start(bf16[2064,128]{1,0:T(8,128)(2,1)S(1)} %pad_maximum_fusion), channel_id=1, source_target_pairs={{0,1},{1,0},{2,3},{3,2},{4,5},{5,4},{6,7},{7,6},{8,9},{9,8},{10,11... | collective-permute-start | bytes 1585160 | tf_op jit(solution)/shard_map/ppermute | solution.py:257
  59.4 30.3 %copy-start = (bf16[1024,256]{1,0:T(8,128)(2,1)S(1)}, bf16[1024,256]{1,0:T(8,128)(2,1)}, u32[]{:S(2)}) copy-start(bf16[1024,256]{1,0:T(8,128)(2,1)} %w_ref.1) | copy-start | bytes 1572868
  60.8 6.2 %copy-start.3 = (bf16[32,8,256]{2,1,0:T(8,128)(2,1)S(1)}, bf16[32,8,256]{2,1,0:T(8,128)(2,1)}, u32[]{:S(2)}) copy-start(bf16[32,8,256]{2,1,0:T(8,128)(2,1)} %get-tuple-element.14.own_ref) | copy-start | bytes 393220
  60.8 28.8 %all-to-all-start.1 = ((bf16[32,8,1280]{2,1,0:T(8,128)(2,1)}), bf16[32,8,1280]{2,1,0:T(8,128)(2,1)S(1)}, u32[]{:S(2)}, u32[]{:S(2)}) async-start(bf16[32,8,1280]{2,1,0:T(8,128)(2,1)} %get-tuple-element.13), calls=%async_computation.1 | async-start | bytes 1310720 | tf_op jit(solution)/shard_map/all_to_all | solution.py:237
  67.0 3.2 %collective-permute-start.1 = (bf16[32,8,256]{2,1,0:T(8,128)(2,1)S(1)}, bf16[32,8,256]{2,1,0:T(8,128)(2,1)S(1)}, u32[]{:S(2)}, u32[]{:S(2)}) collective-permute-start(bf16[32,8,256]{2,1,0:T(8,128)(2,1)S(1)} %copy-done.3), channel_id=1, source_target_pairs={{0,1},{1,0},{2,3},{3,2},{4,5},{5,4},{6,7},{7,6},{8,9},{9,8},{10,11... | collective-permute-start | bytes 393224 | tf_op jit(solution)/shard_map/ppermute | solution.py:300

commit v3 on v2

--- a/solution.py
+++ b/solution.py
@@ -15,11 +15,12 @@
 SPAN = 512
 BLOCK = 4
 STEPS = 4
-SEQ = ("seq_0", "seq_1")
-SEQ_GROUP = ("seq_0", "seq_1", "group")
-SEQ_TENSOR = ("seq_0", "seq_1", "tensor")
+SEQ = ("seq_0", "seq_1", "pair")
+SEQ_GROUP = (*SEQ, "group")
+SEQ_TENSOR = (*SEQ, "tensor")
 
 PEERS = 32
+MATES = PEERS // 2
 LOCAL = 8
 ROWS = 16
 SLOTS = 256
@@ -123,9 +124,10 @@
     values[2 * CACHED :, :] = jnp.zeros((HEAD, HEAD), bf16)
     keys[2 * CACHED : 2 * CACHED + 16, :] = near_k.astype(bf16)
     values[2 * CACHED : 2 * CACHED + 16, :] = near_v.astype(bf16)
-    out_ref[:, :, DEC:NEW] = dec_ref[:, :, 0 : 2 * HEAD]
-    out_ref[:, :, NEW : NEW + HEAD] = jnp.broadcast_to(own_k[None], (PEERS, 8, HEAD)).astype(bf16)
-    out_ref[:, :, NEW + HEAD :] = jnp.broadcast_to(own_v[None], (PEERS, 8, HEAD)).astype(bf16)
+    for a in range(2):
+        out_ref[:, a, :, DEC:NEW] = dec_ref[:, a, :, 0 : 2 * HEAD]
+        out_ref[:, a, :, NEW : NEW + HEAD] = jnp.broadcast_to(own_k[None], (MATES, 8, HEAD)).astype(bf16)
+        out_ref[:, a, :, NEW + HEAD :] = jnp.broadcast_to(own_v[None], (MATES, 8, HEAD)).astype(bf16)
 
     lane = lax.broadcasted_iota(jnp.int32, (PEERS, 8, HEAD), 2)
     index = lax.broadcasted_iota(jnp.int32, (HALF, HEAD), 1)
@@ -138,7 +140,7 @@
         return jnp.concatenate([s[:, : 2 * CACHED], jnp.where(seen, s[:, 2 * CACHED :], NEG)], axis=1)
 
     upcoming = scores(0)
-    stat = dec_ref[:, :, 2 * HEAD :].astype(f32)
+    stat = jnp.concatenate([dec_ref[:, a, :, 2 * HEAD :].astype(f32) for a in range(2)], axis=0)
     for h in range(LOCAL):
         s = upcoming
         if h + 1 < LOCAL:
@@ -150,11 +152,13 @@
         total = jnp.sum(p, axis=1, keepdims=True)
         o = dot(p.astype(bf16), values[...])
         o = (o / total).reshape(PEERS, 8, HEAD)
-        out_ref[:, :, h * HEAD : (h + 1) * HEAD] = o.astype(bf16)
+        for a in range(2):
+            out_ref[:, a, :, h * HEAD : (h + 1) * HEAD] = o[a * MATES : (a + 1) * MATES].astype(bf16)
         logs = jnp.broadcast_to(log_total(peak, total), (HALF, HEAD)).reshape(PEERS, 8, HEAD)
         for i, term in enumerate(terms(logs)):
             stat = jnp.where(lane == 3 * h + i, term, stat)
-    out_ref[:, :, STAT:DEC] = stat.astype(bf16)
+    for a in range(2):
+        out_ref[:, a, :, STAT:DEC] = stat[a * MATES : (a + 1) * MATES].astype(bf16)
 
 
 def combine_kernel(in_ref, out_ref, new_ref):
@@ -169,27 +173,36 @@
         at = j * HEAD if j < LOCAL else DEC + (j - LOCAL) * HEAD
         x = in_ref[:, :, at : at + HEAD].astype(f32)
         total = jnp.sum(x * share[:, :, lane : lane + 1], axis=0)
-        out_ref[:, :, j * HEAD : (j + 1) * HEAD] = jnp.broadcast_to(total[None], (PEERS, 8, HEAD)).astype(bf16)
-
-
-def project_kernel(in_ref, w_ref, out_ref, rows):
-    rows[0:HALF, :] = in_ref[:, :, 0:STAT].astype(f32).reshape(HALF, STAT)
+        out_ref[:, :, j * HEAD : (j + 1) * HEAD] = jnp.broadcast_to(total[None], (MATES, 8, HEAD)).astype(bf16)
+
+
+def project_kernel(in_ref, w_ref, far_ref, out_ref, rows):
+    pair = lax.axis_index("pair")
+    rows[0 : HALF // 2, :] = in_ref[:, :, 0:STAT].astype(f32).reshape(HALF // 2, STAT)
     for h in range(LOCAL):
-        for t in range(STEPS):
+        for t in range(STEPS // 2):
             for b in range(2):
-                at = HALF + t * ROWS + b * 8
-                x = in_ref[h * STEPS + t, :, STAT + b * HEAD : STAT + (b + 1) * HEAD]
+                at = HALF // 2 + t * ROWS + b * 8
+                x = in_ref[h * STEPS // 2 + t, :, STAT + b * HEAD : STAT + (b + 1) * HEAD]
                 rows[at : at + 8, h * HEAD : (h + 1) * HEAD] = x.astype(f32)
-    y = dot(rows[...].astype(bf16), w_ref[...])
-    y = jnp.concatenate([y, jnp.zeros((HEAD // 2, y.shape[1]), f32)], axis=0)
-    y = y.T
-    out_ref[...] = y.reshape(8, 32, 3 * HEAD).astype(bf16)
+    x = rows[...].astype(bf16)
+
+    def projected(ref):
+        y = dot(x, ref[...])
+        y = jnp.concatenate([y, jnp.zeros((2 * HEAD - y.shape[0], y.shape[1]), f32)], axis=0)
+        return y.T.reshape(8, 32, 2 * HEAD).astype(bf16)
+
+    out_ref[pl.ds(pl.multiple_of(pair * 8, 8), 8)] = projected(w_ref)
+    out_ref[pl.ds(pl.multiple_of((1 - pair) * 8, 8), 8)] = projected(far_ref)
 
 
 def last_kernel(in_ref, prefill_ref, decode_ref):
-    y = jnp.sum(in_ref[...].astype(f32), axis=0)
-    prefill_ref[...] = y[:, 0:HALF].astype(bf16)
-    decode_ref[...] = y[:, HALF : HALF + HEAD].T[: STEPS * ROWS].reshape(STEPS, ROWS, 32).astype(bf16)
+    for a in range(2):
+        y = jnp.sum(in_ref[a * 8 : (a + 1) * 8].astype(f32), axis=0)
+        prefill_ref[:, a * HEAD : (a + 1) * HEAD] = y[:, 0:HEAD].astype(bf16)
+        steps = y[:, HEAD : 2 * HEAD].T
+        for t in range(STEPS // 2):
+            decode_ref[2 * t + a] = steps[t * ROWS : (t + 1) * ROWS].astype(bf16)
 
 
 def landing_kernel(row_ref, own_ref, far_ref, keys_ref, values_ref):
@@ -255,6 +268,7 @@
 ):
     mine = jnp.concatenate([cached_keys, cached_values, span_keys, span_values], axis=0)
     other = lax.ppermute(mine, "group", [(0, 1), (1, 0)])
+    far_weight = lax.ppermute(out_weight, "pair", [(0, 1), (1, 0)])
 
     lines = LOCAL * STEPS * ROWS
     decoded = pl.pallas_call(
@@ -270,7 +284,7 @@
     packed = pl.pallas_call(
         prefill_kernel,
         name="prefill",
-        out_shape=jax.ShapeDtypeStruct((PEERS, 8, WIDE), bf16),
+        out_shape=jax.ShapeDtypeStruct((MATES, 2, 8, WIDE), bf16),
         in_specs=[VMEM] * 7,
         out_specs=VMEM,
         scratch_shapes=[pltpu.VMEM((KEYS, HEAD), bf16)] * 2,
@@ -282,15 +296,16 @@
         span_keys,
         span_values,
         near(other),
-        decoded,
-    )
-
-    arrived = swap(packed, SEQ)
+        decoded.reshape(MATES, 2, 8, 3 * HEAD),
+    )
+
+    packed, far_weight = lax.optimization_barrier((packed, far_weight))
+    arrived = swap(packed.reshape(PEERS, 8, WIDE), SEQ)
     attention, new_own = pl.pallas_call(
         combine_kernel,
         name="combine",
         out_shape=(
-            jax.ShapeDtypeStruct((PEERS, 8, THIN), bf16),
+            jax.ShapeDtypeStruct((MATES, 8, THIN), bf16),
             jax.ShapeDtypeStruct((PEERS, 8, 2 * HEAD), bf16),
         ),
         in_specs=[VMEM],
@@ -298,7 +313,7 @@
         cost_estimate=cost(1 << 20, 2 << 20),
     )(near(arrived))
     new_far = lax.ppermute(new_own, "group", [(0, 1), (1, 0)])
-    attention = swap(attention, SEQ)
+    attention = swap(attention, SEQ[:2])
     landed_keys, landed_values = pl.pallas_call(
         landing_kernel,
         name="landing",
@@ -312,13 +327,13 @@
     partial = pl.pallas_call(
         project_kernel,
         name="project",
-        out_shape=jax.ShapeDtypeStruct((8, columns // 8, 3 * HEAD), bf16),
-        in_specs=[VMEM] * 2,
+        out_shape=jax.ShapeDtypeStruct((16, columns // 8, 2 * HEAD), bf16),
+        in_specs=[VMEM] * 3,
         out_specs=VMEM,
-        scratch_shapes=[pltpu.VMEM((HALF + STEPS * ROWS, STAT), f32)],
+        scratch_shapes=[pltpu.VMEM(((HALF + STEPS * ROWS) // 2, STAT), f32)],
         cost_estimate=cost(2 * 320 * STAT * columns, 2 << 20),
-    )(near(attention), near(out_weight))
-    partial = swap(partial, "tensor")
+    )(near(attention), out_weight, near(far_weight))
+    partial = swap(partial, ("pair", "tensor"))
     prefill_out, decode_out = pl.pallas_call(
         last_kernel,
         name="last",
@@ -336,8 +351,8 @@
 
 def solution(mesh):
     torus = Mesh(
-        mesh.devices.reshape(4, 8, mesh.shape["tensor"], mesh.shape["group"]),
-        ("seq_0", "seq_1", "tensor", "group"),
+        mesh.devices.reshape(4, 4, 2, mesh.shape["tensor"], mesh.shape["group"]),
+        (*SEQ, "tensor", "group"),
     )
     in_specs = (
         P(None, "tensor"),

time: 104 us -> 100 us (0.962)
  waiting for transfers between devices: 19.1 us -> 11.8 us
  starting transfers between devices: 10.1 us -> 15.3 us
  blocking collectives: 55.6 us -> 52.3 us
    all_to_all x1, waiting for transfers between devices: 17.8 us -> 9.37 us  [swap(): return lax.all_to_all(x, axis, 0, 0, tiled=True)]
    ppermute x0 -> x1, starting transfers between devices: none -> 7.71 us  [body(): far_weight = lax.ppermute(out_weight, 'pair', [(0, 1), (1, 0)])]
    all_to_all x2, blocking collectives: 55.6 us -> 52.3 us  [swap(): return lax.all_to_all(x, axis, 0, 0, tiled=True)]
    all_to_all x1, starting transfers between devices: 6.17 us -> 3.58 us  [swap(): return lax.all_to_all(x, axis, 0, 0, tiled=True)]
    pallas_call x1, Pallas kernels: 1.11 us -> 2.22 us  [body(): pl.pallas_call(project_kernel, name='project', out_shape=jax.ShapeDtypeSt...]
  transfers between devices with their start and end apart: 3 -> 4, of which waited for: 2 -> 3; matrix products, arithmetic and copies ran while one was open for 0% -> 0% of each run, Pallas kernels for 5% -> 13%
where the time goes in v3:
time: 100 us; the launch traced here: 99.8 us
  blocking collectives  52.3 us (52%)
  Pallas kernels  17.7 us (18%)
  starting transfers between devices  15.3 us (15%)
  waiting for transfers between devices  11.8 us (12%)
  other arithmetic  1.1 us (1%)
    all_to_all x2, blocking collectives, swap(): return lax.all_to_all(x, axis, 0, 0, tiled=True)  52.3 us
    all_to_all x1, waiting for transfers between devices, swap(): return lax.all_to_all(x, axis, 0, 0, tiled=True)  9.37 us
    pallas_call x1, Pallas kernels, body(): pl.pallas_call(prefill_kernel, name='prefill', out_shape=jax.ShapeDtypeSt...  8.47 us
    ppermute x1, starting transfers between devices, body(): far_weight = lax.ppermute(out_weight, 'pair', [(0, 1), (1, 0)])  7.71 us
    all_to_all x1, starting transfers between devices, swap(): return lax.all_to_all(x, axis, 0, 0, tiled=True)  3.58 us
    pallas_call x1, Pallas kernels, body(): pl.pallas_call(decode_kernel, name='decode', out_shape=jax.ShapeDtypeStru...  3.37 us
    pallas_call x1, Pallas kernels, body(): pl.pallas_call(project_kernel, name='project', out_shape=jax.ShapeDtypeSt...  2.22 us
    ppermute x1, starting transfers between devices, body(): other = lax.ppermute(mine, 'group', [(0, 1), (1, 0)])  2.05 us
  transfers between devices with their start and end apart: 4, of which 3 were waited for; matrix products, arithmetic and copies ran while one was open for 0% of the time, Pallas kernels for 13%

profile of v3, /device:TPU:8, one launch (start us, length us, event | category | flops | bytes accessed | tf_op | source)
XLA Modules:
  0.0 99.8 jit_solution(13819450482949203147)
XLA Ops:
  0.6 1.1 %pad_maximum_fusion = bf16[2064,128]{1,0:T(8,128)(2,1)S(1)} fusion(bf16[8,128]{1,0:T(8,128)(2,1)} %sv_ref.1, bf16[8,128]{1,0:T(8,128)(2,1)} %sk_ref.1, bf16[1024,128]{1,0:T(8,128)(2,1)} %v_ref.3, bf16[1024,128]{1,0:T(8,128)(2,1)} %k_ref.3), kind=kLoop, calls=%fused_computation | loop fusion | flops 2113536 | bytes 1056768 | tf_op jit(solution)/shard_map/concatenate | solution.py:269
  1.7 0.0 copy-start
  1.7 0.0 copy-start.1
  1.8 0.0 copy-start.3
  1.8 2.1 %collective-permute-start = (bf16[2064,128]{1,0:T(8,128)(2,1)S(1)}, bf16[2064,128]{1,0:T(8,128)(2,1)S(1)}, u32[]{:S(2)}, u32[]{:S(2)}) collective-permute-start(bf16[2064,128]{1,0:T(8,128)(2,1)S(1)} %pad_maximum_fusion), channel_id=1, source_target_pairs={{0,1},{1,0},{2,3},{3,2},{4,5},{5,4},{6,7},{7,6},{8,9},{9,8},{10,11... | collective-permute-start | bytes 1585160 | tf_op jit(solution)/shard_map/ppermute | solution.py:270
  3.8 7.7 %collective-permute-start.1 = (bf16[1024,256]{1,0:T(8,128)(2,1)}, bf16[1024,256]{1,0:T(8,128)(2,1)S(1)}, u32[]{:S(2)}, u32[]{:S(2)}) collective-permute-start(bf16[1024,256]{1,0:T(8,128)(2,1)} %w_ref.1), channel_id=1, source_target_pairs={{0,16},{16,0},{1,17},{17,1},{2,18},{18,2},{3,19},{19,3},{4,20},{20... | collective-permute-start | bytes 1572872 | tf_op jit(solution)/shard_map/ppermute | solution.py:271
  11.5 3.4 %decode.1 = bf16[32,8,384]{2,1,0:T(8,128)(2,1)} custom-call(s32[32]{0:T(128)} %lengths.1, s32[16]{0:T(128)} %requests.1, bf16[4,16,1024]{2,1,0:T(8,128)(2,1)} %q_ref.2, bf16[16,256,128]{2,1,0:T(8,128)(2,1)} %k_ref.2, bf16[16,256,128]{2,1,0:T(8,128)(2,1)} %v_ref.2, bf16[4,16,128]{2,1,0:T(8,128)(2,1)} %nk_ref.1, bf16[4,16,128]{2,1,0:T(8,128)(2,1)} %nv_ref.1), custom_call_target="tpu_custom_call" | custom-call | flops 536870912 | bytes 3145728 | tf_op jit(solution)/shard_map/decode/pallas_call | solution.py:274
  14.9 0.0 collective-permute-done.other_ref
  14.9 0.0 copy-done
  14.9 0.0 copy-done.1
  14.9 0.0 copy-done.3
  14.9 8.5 %prefill.1 = bf16[16,2,8,1664]{3,2,1,0:T(8,128)(2,1)} custom-call(bf16[512,1024]{1,0:T(8,128)(2,1)S(1)} %copy-done.3, bf16[1024,128]{1,0:T(8,128)(2,1)S(1)} %copy-done, bf16[1024,128]{1,0:T(8,128)(2,1)S(1)} %copy-done.1, bf16[8,128]{1,0:T(8,128)(2,1)} %sk_ref.1, bf16[8,128]{1,0:T(8,128)(2,1)} %sv_ref.1, ...), custom_call_target="tpu_custom_call" | custom-call | flops 2281701376 | bytes 4194304 | tf_op jit(solution)/shard_map/prefill/pallas_call | solution.py:284
  23.4 0.9 collective-permute-done.1.far_ref
  24.3 38.9 %all_to_all.15.in_ref = bf16[32,8,1664]{2,1,0:T(8,128)(2,1)S(1)} all-to-all(bf16[32,8,1664]{2,1,0:T(8,128)(2,1)} %bitcast.6), channel_id=1, replica_groups=mesh['seq_0'=4,'seq_1'=4,'pair'=2,'tensor'=8,'group'=2] {'seq_0','seq_1'..., dimensions={0} | all-to-all | bytes 1703936 | tf_op jit(solution)/shard_map/all_to_all | solution.py:250
  63.3 1.3 %combine.1 = (bf16[16,8,1280]{2,1,0:T(8,128)(2,1)}, bf16[32,8,256]{2,1,0:T(8,128)(2,1)}) custom-call(bf16[32,8,1664]{2,1,0:T(8,128)(2,1)S(1)} %all_to_all.15.in_ref), custom_call_target="tpu_custom_call" | custom-call | flops 1048576 | bytes 2097152 | tf_op jit(solution)/shard_map/combine/pallas_call | solution.py:304
  64.6 3.6 %all-to-all-start.1 = ((bf16[16,8,1280]{2,1,0:T(8,128)(2,1)}), bf16[16,8,1280]{2,1,0:T(8,128)(2,1)S(1)}, u32[]{:S(2)}, u32[]{:S(2)}) async-start(bf16[16,8,1280]{2,1,0:T(8,128)(2,1)} %get-tuple-element.16), calls=%async_computation.1 | async-start | bytes 655360 | tf_op jit(solution)/shard_map/all_to_all | solution.py:250
  68.2 1.9 %collective-permute-start.2 = (bf16[32,8,256]{2,1,0:T(8,128)(2,1)}, bf16[32,8,256]{2,1,0:T(8,128)(2,1)S(1)}, u32[]{:S(2)}, u32[]{:S(2)}) collective-permute-start(bf16[32,8,256]{2,1,0:T(8,128)(2,1)} %get-tuple-element.17.own_ref), channel_id=1, source_target_pairs={{0,1},{1,0},{2,3},{3,2},{4,5},{5,4},{6,7},{7,6},{8,9},{9,8},{10,11... | collective-permute-start | bytes 393224 | tf_op jit(solution)/shard_map/ppermute | solution.py:315
  70.1 1.5 %collective-permute-done.2.far_ref = bf16[32,8,256]{2,1,0:T(8,128)(2,1)S(1)} collective-permute-done((bf16[32,8,256]{2,1,0:T(8,128)(2,1)}, bf16[32,8,256]{2,1,0:T(8,128)(2,1)S(1)}, u32[]{:S(2)}, u32[]{:S(2)}) %collective-permute-start.2) | collective-permute-done | bytes 131104 | tf_op jit(solution)/shard_map/ppermute | solution.py:315
  71.6 0.0 copy-start.2
  71.6 0.9 copy-done.2
  72.5 1.6 %landing.1 = (bf16[16,128]{1,0:T(8,128)(2,1)}, bf16[16,128]{1,0:T(8,128)(2,1)}) custom-call(s32[1,128]{1,0:T(1,128)} %bitcast.8, bf16[32,8,256]{2,1,0:T(8,128)(2,1)S(1)} %copy-done.2, bf16[32,8,256]{2,1,0:T(8,128)(2,1)S(1)} %collective-permute-done.2.far_ref), custom_call_target="tpu_custom_call" | custom-call | flops 4194304 | bytes 524288 | tf_op jit(solution)/shard_map/landing/pallas_call | solution.py:317
  74.1 9.4 %all-to-all-done.1.in_ref = bf16[16,8,1280]{2,1,0:T(8,128)(2,1)S(1)} async-done(((bf16[16,8,1280]{2,1,0:T(8,128)(2,1)}), bf16[16,8,1280]{2,1,0:T(8,128)(2,1)S(1)}, u32[]{:S(2)}, u32[]{:S(2)}) %all-to-all-start.1) | async-done | bytes 327712 | tf_op jit(solution)/shard_map/all_to_all | solution.py:250
  83.5 2.2 %project.1 = bf16[16,32,256]{2,1,0:T(8,128)(2,1)} custom-call(bf16[16,8,1280]{2,1,0:T(8,128)(2,1)S(1)} %all-to-all-done.1.in_ref, bf16[1024,256]{1,0:T(8,128)(2,1)} %w_ref.1, bf16[1024,256]{1,0:T(8,128)(2,1)S(1)} %collective-permute-done.1.far_ref), custom_call_target="tpu_custom_call" | custom-call | flops 167772160 | bytes 2097152 | tf_op jit(solution)/shard_map/project/pallas_call | solution.py:327
  85.7 13.4 %all_to_all.16.in_ref = bf16[16,32,256]{2,1,0:T(8,128)(2,1)S(1)} all-to-all(bf16[16,32,256]{2,1,0:T(8,128)(2,1)} %project.1), channel_id=1, replica_groups=mesh['seq_0'=4,'seq_1'=4,'pair'=2,'tensor'=8,'group'=2] {'pair','tensor'}, dimensions={0} | all-to-all | bytes 524288 | tf_op jit(solution)/shard_map/all_to_all | solution.py:250
  99.1 0.7 last.1
Async XLA Ops:
  1.7 13.2 %copy-start = (bf16[1024,128]{1,0:T(8,128)(2,1)S(1)}, bf16[1024,128]{1,0:T(8,128)(2,1)}, u32[]{:S(2)}) copy-start(bf16[1024,128]{1,0:T(8,128)(2,1)} %k_ref.3) | copy-start | bytes 786436
  1.7 13.2 %copy-start.1 = (bf16[1024,128]{1,0:T(8,128)(2,1)S(1)}, bf16[1024,128]{1,0:T(8,128)(2,1)}, u32[]{:S(2)}) copy-start(bf16[1024,128]{1,0:T(8,128)(2,1)} %v_ref.3) | copy-start | bytes 786436
  1.8 13.2 %copy-start.3 = (bf16[512,1024]{1,0:T(8,128)(2,1)S(1)}, bf16[512,1024]{1,0:T(8,128)(2,1)}, u32[]{:S(2)}) copy-start(bf16[512,1024]{1,0:T(8,128)(2,1)} %q_ref.3) | copy-start | bytes 3145732
  1.8 13.1 %collective-permute-start = (bf16[2064,128]{1,0:T(8,128)(2,1)S(1)}, bf16[2064,128]{1,0:T(8,128)(2,1)S(1)}, u32[]{:S(2)}, u32[]{:S(2)}) collective-permute-start(bf16[2064,128]{1,0:T(8,128)(2,1)S(1)} %pad_maximum_fusion), channel_id=1, source_target_pairs={{0,1},{1,0},{2,3},{3,2},{4,5},{5,4},{6,7},{7,6},{8,9},{9,8},{10,11... | collective-permute-start | bytes 1585160 | tf_op jit(solution)/shard_map/ppermute | solution.py:270
  3.8 20.5 %collective-permute-start.1 = (bf16[1024,256]{1,0:T(8,128)(2,1)}, bf16[1024,256]{1,0:T(8,128)(2,1)S(1)}, u32[]{:S(2)}, u32[]{:S(2)}) collective-permute-start(bf16[1024,256]{1,0:T(8,128)(2,1)} %w_ref.1), channel_id=1, source_target_pairs={{0,16},{16,0},{1,17},{17,1},{2,18},{18,2},{3,19},{19,3},{4,20},{20... | collective-permute-start | bytes 1572872 | tf_op jit(solution)/shard_map/ppermute | solution.py:271
  64.6 18.9 %all-to-all-start.1 = ((bf16[16,8,1280]{2,1,0:T(8,128)(2,1)}), bf16[16,8,1280]{2,1,0:T(8,128)(2,1)S(1)}, u32[]{:S(2)}, u32[]{:S(2)}) async-start(bf16[16,8,1280]{2,1,0:T(8,128)(2,1)} %get-tuple-element.16), calls=%async_computation.1 | async-start | bytes 655360 | tf_op jit(solution)/shard_map/all_to_all | solution.py:250
  68.2 3.5 %collective-permute-start.2 = (bf16[32,8,256]{2,1,0:T(8,128)(2,1)}, bf16[32,8,256]{2,1,0:T(8,128)(2,1)S(1)}, u32[]{:S(2)}, u32[]{:S(2)}) collective-permute-start(bf16[32,8,256]{2,1,0:T(8,128)(2,1)} %get-tuple-element.17.own_ref), channel_id=1, source_target_pairs={{0,1},{1,0},{2,3},{3,2},{4,5},{5,4},{6,7},{7,6},{8,9},{9,8},{10,11... | collective-permute-start | bytes 393224 | tf_op jit(solution)/shard_map/ppermute | solution.py:315
  71.6 0.9 copy-start.2

commit v4 on v3

--- a/solution.py
+++ b/solution.py
@@ -1,4 +1,3 @@
-import functools
 import math
 
 import jax
@@ -9,8 +8,7 @@
 from jax.sharding import Mesh
 from jax.sharding import PartitionSpec as P
 
-HEADS = 64
-KV_HEADS = 8
+
 HEAD = 128
 SPAN = 512
 BLOCK = 4
@@ -190,7 +188,7 @@
     def projected(ref):
         y = dot(x, ref[...])
         y = jnp.concatenate([y, jnp.zeros((2 * HEAD - y.shape[0], y.shape[1]), f32)], axis=0)
-        return y.T.reshape(8, 32, 2 * HEAD).astype(bf16)
+        return y.astype(bf16).T.reshape(8, 32, 2 * HEAD)
 
     out_ref[pl.ds(pl.multiple_of(pair * 8, 8), 8)] = projected(w_ref)
     out_ref[pl.ds(pl.multiple_of((1 - pair) * 8, 8), 8)] = projected(far_ref)
@@ -267,8 +265,8 @@
     block_table,
 ):
     mine = jnp.concatenate([cached_keys, cached_values, span_keys, span_values], axis=0)
+    far_weight = lax.ppermute(out_weight, "pair", [(0, 1), (1, 0)])
     other = lax.ppermute(mine, "group", [(0, 1), (1, 0)])
-    far_weight = lax.ppermute(out_weight, "pair", [(0, 1), (1, 0)])
 
     lines = LOCAL * STEPS * ROWS
     decoded = pl.pallas_call(
@@ -301,6 +299,7 @@
 
     packed, far_weight = lax.optimization_barrier((packed, far_weight))
     arrived = swap(packed.reshape(PEERS, 8, WIDE), SEQ)
+    arrived, late_weight = lax.optimization_barrier((arrived, out_weight))
     attention, new_own = pl.pallas_call(
         combine_kernel,
         name="combine",
@@ -324,6 +323,7 @@
     )(block_table.reshape(1, -1), near(new_own), near(new_far))
     attention, landed_keys, landed_values = lax.optimization_barrier((attention, landed_keys, landed_values))
     columns = out_weight.shape[1]
+    near_weight = near(late_weight)
     partial = pl.pallas_call(
         project_kernel,
         name="project",
@@ -332,7 +332,7 @@
         out_specs=VMEM,
         scratch_shapes=[pltpu.VMEM(((HALF + STEPS * ROWS) // 2, STAT), f32)],
         cost_estimate=cost(2 * 320 * STAT * columns, 2 << 20),
-    )(near(attention), out_weight, near(far_weight))
+    )(near(attention), near_weight, near(far_weight))
     partial = swap(partial, ("pair", "tensor"))
     prefill_out, decode_out = pl.pallas_call(
         last_kernel,

time: 100 us -> 100 us (level)
  the two profiles are of different devices: /device:TPU:8 before, /device:TPU:2 now
where the time goes in v4:
time: 100 us; the launch traced here: 99.4 us
  blocking collectives  53.7 us (54%)
  Pallas kernels  16.6 us (17%)
  starting transfers between devices  14.3 us (14%)
  waiting for transfers between devices  11.2 us (11%)
  other arithmetic  1.96 us (2%)
    all_to_all x2, blocking collectives, swap(): return lax.all_to_all(x, axis, 0, 0, tiled=True)  53.7 us
    all_to_all x1, waiting for transfers between devices, swap(): return lax.all_to_all(x, axis, 0, 0, tiled=True)  8.83 us
    pallas_call x1, Pallas kernels, body(): pl.pallas_call(prefill_kernel, name='prefill', out_shape=jax.ShapeDtypeSt...  8.47 us
    all_to_all x1, starting transfers between devices, swap(): return lax.all_to_all(x, axis, 0, 0, tiled=True)  6.86 us
    ppermute x1, starting transfers between devices, body(): far_weight = lax.ppermute(out_weight, 'pair', [(0, 1), (1, 0)])  3.48 us
    pallas_call x1, Pallas kernels, body(): pl.pallas_call(decode_kernel, name='decode', out_shape=jax.ShapeDtypeStru...  3.38 us
    ppermute x1, starting transfers between devices, body(): other = lax.ppermute(mine, 'group', [(0, 1), (1, 0)])  2.05 us
  transfers between devices with their start and end apart: 4, of which 3 were waited for; matrix products, arithmetic and copies ran while one was open for 0% of the time, Pallas kernels for 14%

profile of v4, /device:TPU:2, one launch (start us, length us, event | category | flops | bytes accessed | tf_op | source)
XLA Modules:
  0.0 99.4 jit_solution(2542381293142696608)
XLA Ops:
  0.6 0.0 copy-start
  0.6 2.0 %pad_maximum_fusion = bf16[2064,128]{1,0:T(8,128)(2,1)} fusion(bf16[8,128]{1,0:T(8,128)(2,1)} %sv_ref.1, bf16[8,128]{1,0:T(8,128)(2,1)} %sk_ref.1, bf16[1024,128]{1,0:T(8,128)(2,1)} %v_ref.3, bf16[1024,128]{1,0:T(8,128)(2,1)} %k_ref.3), kind=kLoop, calls=%fused_computation | loop fusion | flops 2113536 | bytes 1056768 | tf_op jit(solution)/shard_map/concatenate | solution.py:267
  2.6 0.0 copy-start.1
  2.6 0.0 copy-start.2
  2.6 0.0 copy-start.4
  2.6 2.0 %collective-permute-start = (bf16[2064,128]{1,0:T(8,128)(2,1)}, bf16[2064,128]{1,0:T(8,128)(2,1)S(1)}, u32[]{:S(2)}, u32[]{:S(2)}) collective-permute-start(bf16[2064,128]{1,0:T(8,128)(2,1)} %pad_maximum_fusion), channel_id=1, source_target_pairs={{0,1},{1,0},{2,3},{3,2},{4,5},{5,4},{6,7},{7,6},{8,9},{9,8},{10,11... | collective-permute-start | bytes 1585160 | tf_op jit(solution)/shard_map/ppermute | solution.py:269
  4.7 0.0 copy-done
  4.7 3.5 %collective-permute-start.1 = (bf16[1024,256]{1,0:T(8,128)(2,1)S(1)}, bf16[1024,256]{1,0:T(8,128)(2,1)S(1)}, u32[]{:S(2)}, u32[]{:S(2)}) collective-permute-start(bf16[1024,256]{1,0:T(8,128)(2,1)S(1)} %copy-done), channel_id=1, source_target_pairs={{0,16},{16,0},{1,17},{17,1},{2,18},{18,2},{3,19},{19,3},{4,20},{20... | collective-permute-start | bytes 1572872 | tf_op jit(solution)/shard_map/ppermute | solution.py:268
  8.2 3.4 %decode.1 = bf16[32,8,384]{2,1,0:T(8,128)(2,1)} custom-call(s32[32]{0:T(128)} %lengths.1, s32[16]{0:T(128)} %requests.1, bf16[4,16,1024]{2,1,0:T(8,128)(2,1)} %q_ref.2, bf16[16,256,128]{2,1,0:T(8,128)(2,1)} %k_ref.2, bf16[16,256,128]{2,1,0:T(8,128)(2,1)} %v_ref.2, bf16[4,16,128]{2,1,0:T(8,128)(2,1)} %nk_ref.1, bf16[4,16,128]{2,1,0:T(8,128)(2,1)} %nv_ref.1), custom_call_target="tpu_custom_call" | custom-call | flops 536870912 | bytes 3145728 | tf_op jit(solution)/shard_map/decode/pallas_call | solution.py:272
  11.5 0.0 collective-permute-done.other_ref
  11.5 0.0 copy-done.1
  11.6 0.0 copy-done.2
  11.6 0.0 copy-done.4
  11.6 8.5 %prefill.1 = bf16[16,2,8,1664]{3,2,1,0:T(8,128)(2,1)} custom-call(bf16[512,1024]{1,0:T(8,128)(2,1)S(1)} %copy-done.4, bf16[1024,128]{1,0:T(8,128)(2,1)S(1)} %copy-done.1, bf16[1024,128]{1,0:T(8,128)(2,1)S(1)} %copy-done.2, bf16[8,128]{1,0:T(8,128)(2,1)} %sk_ref.1, bf16[8,128]{1,0:T(8,128)(2,1)} %sv_ref.1, ...), custom_call_target="tpu_custom_call" | custom-call | flops 2281701376 | bytes 4194304 | tf_op jit(solution)/shard_map/prefill/pallas_call | solution.py:282
  20.0 0.9 collective-permute-done.1.far_ref
  20.9 41.4 %all_to_all.15.in_ref = bf16[32,8,1664]{2,1,0:T(8,128)(2,1)S(1)} all-to-all(bf16[32,8,1664]{2,1,0:T(8,128)(2,1)} %bitcast.6), channel_id=1, replica_groups=mesh['seq_0'=4,'seq_1'=4,'pair'=2,'tensor'=8,'group'=2] {'seq_0','seq_1'..., dimensions={0} | all-to-all | bytes 1703936 | tf_op jit(solution)/shard_map/all_to_all | solution.py:248
  62.3 1.3 %combine.1 = (bf16[16,8,1280]{2,1,0:T(8,128)(2,1)}, bf16[32,8,256]{2,1,0:T(8,128)(2,1)}) custom-call(bf16[32,8,1664]{2,1,0:T(8,128)(2,1)S(1)} %all_to_all.15.in_ref), custom_call_target="tpu_custom_call" | custom-call | flops 1048576 | bytes 2097152 | tf_op jit(solution)/shard_map/combine/pallas_call | solution.py:303
  63.6 6.9 %all-to-all-start.1 = ((bf16[16,8,1280]{2,1,0:T(8,128)(2,1)}), bf16[16,8,1280]{2,1,0:T(8,128)(2,1)S(1)}, u32[]{:S(2)}, u32[]{:S(2)}) async-start(bf16[16,8,1280]{2,1,0:T(8,128)(2,1)} %get-tuple-element.19), calls=%async_computation.1 | async-start | bytes 655360 | tf_op jit(solution)/shard_map/all_to_all | solution.py:248
  70.5 1.9 %collective-permute-start.2 = (bf16[32,8,256]{2,1,0:T(8,128)(2,1)}, bf16[32,8,256]{2,1,0:T(8,128)(2,1)S(1)}, u32[]{:S(2)}, u32[]{:S(2)}) collective-permute-start(bf16[32,8,256]{2,1,0:T(8,128)(2,1)} %get-tuple-element.20.own_ref), channel_id=1, source_target_pairs={{0,1},{1,0},{2,3},{3,2},{4,5},{5,4},{6,7},{7,6},{8,9},{9,8},{10,11... | collective-permute-start | bytes 393224 | tf_op jit(solution)/shard_map/ppermute | solution.py:314
  72.4 1.5 %collective-permute-done.2.far_ref = bf16[32,8,256]{2,1,0:T(8,128)(2,1)S(1)} collective-permute-done((bf16[32,8,256]{2,1,0:T(8,128)(2,1)}, bf16[32,8,256]{2,1,0:T(8,128)(2,1)S(1)}, u32[]{:S(2)}, u32[]{:S(2)}) %collective-permute-start.2) | collective-permute-done | bytes 131104 | tf_op jit(solution)/shard_map/ppermute | solution.py:314
  74.0 0.0 copy-start.3
  74.0 0.9 copy-done.3
  74.9 1.6 %landing.1 = (bf16[16,128]{1,0:T(8,128)(2,1)}, bf16[16,128]{1,0:T(8,128)(2,1)}) custom-call(s32[1,128]{1,0:T(1,128)} %bitcast.8, bf16[32,8,256]{2,1,0:T(8,128)(2,1)S(1)} %copy-done.3, bf16[32,8,256]{2,1,0:T(8,128)(2,1)S(1)} %collective-permute-done.2.far_ref), custom_call_target="tpu_custom_call" | custom-call | flops 4194304 | bytes 524288 | tf_op jit(solution)/shard_map/landing/pallas_call | solution.py:316
  76.5 8.8 %all-to-all-done.1.in_ref = bf16[16,8,1280]{2,1,0:T(8,128)(2,1)S(1)} async-done(((bf16[16,8,1280]{2,1,0:T(8,128)(2,1)}), bf16[16,8,1280]{2,1,0:T(8,128)(2,1)S(1)}, u32[]{:S(2)}, u32[]{:S(2)}) %all-to-all-start.1) | async-done | bytes 327712 | tf_op jit(solution)/shard_map/all_to_all | solution.py:248
  85.3 1.1 %project.1 = bf16[16,32,256]{2,1,0:T(8,128)(2,1)} custom-call(bf16[16,8,1280]{2,1,0:T(8,128)(2,1)S(1)} %all-to-all-done.1.in_ref, bf16[1024,256]{1,0:T(8,128)(2,1)S(1)} %copy-done, bf16[1024,256]{1,0:T(8,128)(2,1)S(1)} %collective-permute-done.1.far_ref), custom_call_target="tpu_custom_call" | custom-call | flops 167772160 | bytes 2097152 | tf_op jit(solution)/shard_map/project/pallas_call | solution.py:327
  86.4 12.3 %all_to_all.16.in_ref = bf16[16,32,256]{2,1,0:T(8,128)(2,1)S(1)} all-to-all(bf16[16,32,256]{2,1,0:T(8,128)(2,1)} %project.1), channel_id=1, replica_groups=mesh['seq_0'=4,'seq_1'=4,'pair'=2,'tensor'=8,'group'=2] {'pair','tensor'}, dimensions={0} | all-to-all | bytes 524288 | tf_op jit(solution)/shard_map/all_to_all | solution.py:248
  98.7 0.7 last.1
Async XLA Ops:
  0.6 4.0 %copy-start = (bf16[1024,256]{1,0:T(8,128)(2,1)S(1)}, bf16[1024,256]{1,0:T(8,128)(2,1)}, u32[]{:S(2)}) copy-start(bf16[1024,256]{1,0:T(8,128)(2,1)} %w_ref) | copy-start | bytes 1572868
  2.6 8.9 %copy-start.1 = (bf16[1024,128]{1,0:T(8,128)(2,1)S(1)}, bf16[1024,128]{1,0:T(8,128)(2,1)}, u32[]{:S(2)}) copy-start(bf16[1024,128]{1,0:T(8,128)(2,1)} %k_ref.3) | copy-start | bytes 786436
  2.6 9.0 %copy-start.2 = (bf16[1024,128]{1,0:T(8,128)(2,1)S(1)}, bf16[1024,128]{1,0:T(8,128)(2,1)}, u32[]{:S(2)}) copy-start(bf16[1024,128]{1,0:T(8,128)(2,1)} %v_ref.3) | copy-start | bytes 786436
  2.6 9.0 %copy-start.4 = (bf16[512,1024]{1,0:T(8,128)(2,1)S(1)}, bf16[512,1024]{1,0:T(8,128)(2,1)}, u32[]{:S(2)}) copy-start(bf16[512,1024]{1,0:T(8,128)(2,1)} %q_ref.3) | copy-start | bytes 3145732
  2.6 8.9 %collective-permute-start = (bf16[2064,128]{1,0:T(8,128)(2,1)}, bf16[2064,128]{1,0:T(8,128)(2,1)S(1)}, u32[]{:S(2)}, u32[]{:S(2)}) collective-permute-start(bf16[2064,128]{1,0:T(8,128)(2,1)} %pad_maximum_fusion), channel_id=1, source_target_pairs={{0,1},{1,0},{2,3},{3,2},{4,5},{5,4},{6,7},{7,6},{8,9},{9,8},{10,11... | collective-permute-start | bytes 1585160 | tf_op jit(solution)/shard_map/ppermute | solution.py:269
  4.7 16.2 %collective-permute-start.1 = (bf16[1024,256]{1,0:T(8,128)(2,1)S(1)}, bf16[1024,256]{1,0:T(8,128)(2,1)S(1)}, u32[]{:S(2)}, u32[]{:S(2)}) collective-permute-start(bf16[1024,256]{1,0:T(8,128)(2,1)S(1)} %copy-done), channel_id=1, source_target_pairs={{0,16},{16,0},{1,17},{17,1},{2,18},{18,2},{3,19},{19,3},{4,20},{20... | collective-permute-start | bytes 1572872 | tf_op jit(solution)/shard_map/ppermute | solution.py:268
  63.6 21.7 %all-to-all-start.1 = ((bf16[16,8,1280]{2,1,0:T(8,128)(2,1)}), bf16[16,8,1280]{2,1,0:T(8,128)(2,1)S(1)}, u32[]{:S(2)}, u32[]{:S(2)}) async-start(bf16[16,8,1280]{2,1,0:T(8,128)(2,1)} %get-tuple-element.19), calls=%async_computation.1 | async-start | bytes 655360 | tf_op jit(solution)/shard_map/all_to_all | solution.py:248
  70.5 3.5 %collective-permute-start.2 = (bf16[32,8,256]{2,1,0:T(8,128)(2,1)}, bf16[32,8,256]{2,1,0:T(8,128)(2,1)S(1)}, u32[]{:S(2)}, u32[]{:S(2)}) collective-permute-start(bf16[32,8,256]{2,1,0:T(8,128)(2,1)} %get-tuple-element.20.own_ref), channel_id=1, source_target_pairs={{0,1},{1,0},{2,3},{3,2},{4,5},{5,4},{6,7},{7,6},{8,9},{9,8},{10,11... | collective-permute-start | bytes 393224 | tf_op jit(solution)/shard_map/ppermute | solution.py:314
  74.0 0.9 copy-start.3

commit v5 on v4

--- a/solution.py
+++ b/solution.py
@@ -116,12 +116,13 @@
     near_v = jnp.concatenate([jnp.where(first, own_v, far_v), jnp.where(first, far_v, own_v)], axis=0)
     keys[0:CACHED, :] = k_ref[...]
     keys[CACHED : 2 * CACHED, :] = other_ref[0:CACHED, :]
-    values[0:CACHED, :] = v_ref[...]
-    values[CACHED : 2 * CACHED, :] = other_ref[CACHED : 2 * CACHED, :]
+    values[:, HEAD:] = jnp.ones((KEYS, HEAD), bf16)
+    values[0:CACHED, 0:HEAD] = v_ref[...]
+    values[CACHED : 2 * CACHED, 0:HEAD] = other_ref[CACHED : 2 * CACHED, :]
     keys[2 * CACHED :, :] = jnp.zeros((HEAD, HEAD), bf16)
-    values[2 * CACHED :, :] = jnp.zeros((HEAD, HEAD), bf16)
+    values[2 * CACHED :, 0:HEAD] = jnp.zeros((HEAD, HEAD), bf16)
     keys[2 * CACHED : 2 * CACHED + 16, :] = near_k.astype(bf16)
-    values[2 * CACHED : 2 * CACHED + 16, :] = near_v.astype(bf16)
+    values[2 * CACHED : 2 * CACHED + 16, 0:HEAD] = near_v.astype(bf16)
     for a in range(2):
         out_ref[:, a, :, DEC:NEW] = dec_ref[:, a, :, 0 : 2 * HEAD]
         out_ref[:, a, :, NEW : NEW + HEAD] = jnp.broadcast_to(own_k[None], (MATES, 8, HEAD)).astype(bf16)
@@ -147,12 +148,12 @@
         edge = s[:, 2 * CACHED :]
         p = jnp.exp2((s[:, : 2 * CACHED] - peak) * LOG2)
         p = jnp.concatenate([p, jnp.where(seen, jnp.exp2((edge - peak) * LOG2), 0.0)], axis=1)
-        total = jnp.sum(p, axis=1, keepdims=True)
         o = dot(p.astype(bf16), values[...])
+        o, total = o[:, :HEAD], o[:, HEAD:]
         o = (o / total).reshape(PEERS, 8, HEAD)
         for a in range(2):
             out_ref[:, a, :, h * HEAD : (h + 1) * HEAD] = o[a * MATES : (a + 1) * MATES].astype(bf16)
-        logs = jnp.broadcast_to(log_total(peak, total), (HALF, HEAD)).reshape(PEERS, 8, HEAD)
+        logs = log_total(peak, total).reshape(PEERS, 8, HEAD)
         for i, term in enumerate(terms(logs)):
             stat = jnp.where(lane == 3 * h + i, term, stat)
     for a in range(2):
@@ -185,20 +186,23 @@
                 rows[at : at + 8, h * HEAD : (h + 1) * HEAD] = x.astype(f32)
     x = rows[...].astype(bf16)
 
-    def projected(ref):
+    for ref, side in ((w_ref, pair), (far_ref, 1 - pair)):
         y = dot(x, ref[...])
         y = jnp.concatenate([y, jnp.zeros((2 * HEAD - y.shape[0], y.shape[1]), f32)], axis=0)
-        return y.astype(bf16).T.reshape(8, 32, 2 * HEAD)
-
-    out_ref[pl.ds(pl.multiple_of(pair * 8, 8), 8)] = projected(w_ref)
-    out_ref[pl.ds(pl.multiple_of((1 - pair) * 8, 8), 8)] = projected(far_ref)
+        y = y.astype(bf16).T
+        steps = y[:, HEAD:].astype(f32).reshape(8, 4, 8, HEAD)
+        packed = steps[:, 0].reshape(8 * 8, HEAD) + sum(pltpu.roll(steps[:, g].reshape(8 * 8, HEAD), 32 * g, 1) for g in range(1, 4))
+        peers = pl.ds(pl.multiple_of(side * 8, 8), 8)
+        out_ref[peers, 0:32, :] = y[:, :HEAD].reshape(8, 32, HEAD)
+        out_ref[peers, 32:40, :] = packed.reshape(8, 8, HEAD).astype(bf16)
 
 
 def last_kernel(in_ref, prefill_ref, decode_ref):
     for a in range(2):
         y = jnp.sum(in_ref[a * 8 : (a + 1) * 8].astype(f32), axis=0)
-        prefill_ref[:, a * HEAD : (a + 1) * HEAD] = y[:, 0:HEAD].astype(bf16)
-        steps = y[:, HEAD : 2 * HEAD].T
+        prefill_ref[:, a * HEAD : (a + 1) * HEAD] = y[0:32].astype(bf16)
+        steps = [y[32:40]] + [pltpu.roll(y[32:40], HEAD - 32 * g, 1) for g in range(1, 4)]
+        steps = jnp.concatenate(steps, axis=0).T
         for t in range(STEPS // 2):
             decode_ref[2 * t + a] = steps[t * ROWS : (t + 1) * ROWS].astype(bf16)
 
@@ -285,7 +289,7 @@
         out_shape=jax.ShapeDtypeStruct((MATES, 2, 8, WIDE), bf16),
         in_specs=[VMEM] * 7,
         out_specs=VMEM,
-        scratch_shapes=[pltpu.VMEM((KEYS, HEAD), bf16)] * 2,
+        scratch_shapes=[pltpu.VMEM((KEYS, HEAD), bf16), pltpu.VMEM((KEYS, 2 * HEAD), bf16)],
         cost_estimate=cost(4 * HALF * LOCAL * KEYS * HEAD, 4 << 20, HALF * LOCAL * KEYS),
     )(
         near(prefill_queries),
@@ -327,7 +331,7 @@
     partial = pl.pallas_call(
         project_kernel,
         name="project",
-        out_shape=jax.ShapeDtypeStruct((16, columns // 8, 2 * HEAD), bf16),
+        out_shape=jax.ShapeDtypeStruct((16, columns // 8 + 8, HEAD), bf16),
         in_specs=[VMEM] * 3,
         out_specs=VMEM,
         scratch_shapes=[pltpu.VMEM(((HALF + STEPS * ROWS) // 2, STAT), f32)],

time: 100 us -> 99.8 us (level)
  transfers between devices with their start and end apart: 4 -> 4, of which waited for: 3 -> 3; matrix products, arithmetic and copies ran while one was open for 0% -> 0% of each run, Pallas kernels for 14% -> 13%
where the time goes in v5:
time: 99.8 us; the launch traced here: 99.2 us
  blocking collectives  53.4 us (54%)
  Pallas kernels  16.1 us (16%)
  starting transfers between devices  14.3 us (14%)
  waiting for transfers between devices  11.9 us (12%)
  other arithmetic  1.96 us (2%)
    all_to_all x2, blocking collectives, swap(): return lax.all_to_all(x, axis, 0, 0, tiled=True)  53.4 us
    all_to_all x1, waiting for transfers between devices, swap(): return lax.all_to_all(x, axis, 0, 0, tiled=True)  8.83 us
    pallas_call x1, Pallas kernels, body(): pl.pallas_call(prefill_kernel, name='prefill', out_shape=jax.ShapeDtypeSt...  7.8 us
    all_to_all x1, starting transfers between devices, swap(): return lax.all_to_all(x, axis, 0, 0, tiled=True)  6.86 us
    ppermute x1, starting transfers between devices, body(): far_weight = lax.ppermute(out_weight, 'pair', [(0, 1), (1, 0)])  3.48 us
    pallas_call x1, Pallas kernels, body(): pl.pallas_call(decode_kernel, name='decode', out_shape=jax.ShapeDtypeStru...  3.38 us
    ppermute x1, starting transfers between devices, body(): other = lax.ppermute(mine, 'group', [(0, 1), (1, 0)])  2.05 us
  transfers between devices with their start and end apart: 4, of which 3 were waited for; matrix products, arithmetic and copies ran while one was open for 0% of the time, Pallas kernels for 13%

profile of v5, /device:TPU:2, one launch (start us, length us, event | category | flops | bytes accessed | tf_op | source)
XLA Modules:
  0.0 99.2 jit_solution(7519031279240318369)
XLA Ops:
  0.6 0.0 copy-start
  0.6 2.0 %pad_maximum_fusion = bf16[2064,128]{1,0:T(8,128)(2,1)} fusion(bf16[8,128]{1,0:T(8,128)(2,1)} %sv_ref.1, bf16[8,128]{1,0:T(8,128)(2,1)} %sk_ref.1, bf16[1024,128]{1,0:T(8,128)(2,1)} %v_ref.3, bf16[1024,128]{1,0:T(8,128)(2,1)} %k_ref.3), kind=kLoop, calls=%fused_computation | loop fusion | flops 2113536 | bytes 1056768 | tf_op jit(solution)/shard_map/concatenate | solution.py:271
  2.6 0.0 copy-start.1
  2.6 0.0 copy-start.2
  2.6 0.0 copy-start.4
  2.6 2.0 %collective-permute-start = (bf16[2064,128]{1,0:T(8,128)(2,1)}, bf16[2064,128]{1,0:T(8,128)(2,1)S(1)}, u32[]{:S(2)}, u32[]{:S(2)}) collective-permute-start(bf16[2064,128]{1,0:T(8,128)(2,1)} %pad_maximum_fusion), channel_id=1, source_target_pairs={{0,1},{1,0},{2,3},{3,2},{4,5},{5,4},{6,7},{7,6},{8,9},{9,8},{10,11... | collective-permute-start | bytes 1585160 | tf_op jit(solution)/shard_map/ppermute | solution.py:273
  4.7 0.0 copy-done
  4.7 3.5 %collective-permute-start.1 = (bf16[1024,256]{1,0:T(8,128)(2,1)S(1)}, bf16[1024,256]{1,0:T(8,128)(2,1)S(1)}, u32[]{:S(2)}, u32[]{:S(2)}) collective-permute-start(bf16[1024,256]{1,0:T(8,128)(2,1)S(1)} %copy-done), channel_id=1, source_target_pairs={{0,16},{16,0},{1,17},{17,1},{2,18},{18,2},{3,19},{19,3},{4,20},{20... | collective-permute-start | bytes 1572872 | tf_op jit(solution)/shard_map/ppermute | solution.py:272
  8.2 3.4 %decode.1 = bf16[32,8,384]{2,1,0:T(8,128)(2,1)} custom-call(s32[32]{0:T(128)} %lengths.1, s32[16]{0:T(128)} %requests.1, bf16[4,16,1024]{2,1,0:T(8,128)(2,1)} %q_ref.2, bf16[16,256,128]{2,1,0:T(8,128)(2,1)} %k_ref.2, bf16[16,256,128]{2,1,0:T(8,128)(2,1)} %v_ref.2, bf16[4,16,128]{2,1,0:T(8,128)(2,1)} %nk_ref.1, bf16[4,16,128]{2,1,0:T(8,128)(2,1)} %nv_ref.1), custom_call_target="tpu_custom_call" | custom-call | flops 536870912 | bytes 3145728 | tf_op jit(solution)/shard_map/decode/pallas_call | solution.py:276
  11.5 0.0 collective-permute-done.other_ref
  11.5 0.0 copy-done.1
  11.6 0.0 copy-done.2
  11.6 0.0 copy-done.4
  11.6 7.8 %prefill.1 = bf16[16,2,8,1664]{3,2,1,0:T(8,128)(2,1)} custom-call(bf16[512,1024]{1,0:T(8,128)(2,1)S(1)} %copy-done.4, bf16[1024,128]{1,0:T(8,128)(2,1)S(1)} %copy-done.1, bf16[1024,128]{1,0:T(8,128)(2,1)S(1)} %copy-done.2, bf16[8,128]{1,0:T(8,128)(2,1)} %sk_ref.1, bf16[8,128]{1,0:T(8,128)(2,1)} %sv_ref.1, ...), custom_call_target="tpu_custom_call" | custom-call | flops 2281701376 | bytes 4194304 | tf_op jit(solution)/shard_map/prefill/pallas_call | solution.py:286
  19.4 1.5 %collective-permute-done.1.far_ref = bf16[1024,256]{1,0:T(8,128)(2,1)S(1)} collective-permute-done((bf16[1024,256]{1,0:T(8,128)(2,1)S(1)}, bf16[1024,256]{1,0:T(8,128)(2,1)S(1)}, u32[]{:S(2)}, u32[]{:S(2)}) %collective-permute-start.1) | collective-permute-done | bytes 524320 | tf_op jit(solution)/shard_map/ppermute | solution.py:272
  20.9 41.4 %all_to_all.15.in_ref = bf16[32,8,1664]{2,1,0:T(8,128)(2,1)S(1)} all-to-all(bf16[32,8,1664]{2,1,0:T(8,128)(2,1)} %bitcast.6), channel_id=1, replica_groups=mesh['seq_0'=4,'seq_1'=4,'pair'=2,'tensor'=8,'group'=2] {'seq_0','seq_1'..., dimensions={0} | all-to-all | bytes 1703936 | tf_op jit(solution)/shard_map/all_to_all | solution.py:252
  62.3 1.3 %combine.1 = (bf16[16,8,1280]{2,1,0:T(8,128)(2,1)}, bf16[32,8,256]{2,1,0:T(8,128)(2,1)}) custom-call(bf16[32,8,1664]{2,1,0:T(8,128)(2,1)S(1)} %all_to_all.15.in_ref), custom_call_target="tpu_custom_call" | custom-call | flops 1048576 | bytes 2097152 | tf_op jit(solution)/shard_map/combine/pallas_call | solution.py:307
  63.6 6.9 %all-to-all-start.1 = ((bf16[16,8,1280]{2,1,0:T(8,128)(2,1)}), bf16[16,8,1280]{2,1,0:T(8,128)(2,1)S(1)}, u32[]{:S(2)}, u32[]{:S(2)}) async-start(bf16[16,8,1280]{2,1,0:T(8,128)(2,1)} %get-tuple-element.19), calls=%async_computation.1 | async-start | bytes 655360 | tf_op jit(solution)/shard_map/all_to_all | solution.py:252
  70.5 1.9 %collective-permute-start.2 = (bf16[32,8,256]{2,1,0:T(8,128)(2,1)}, bf16[32,8,256]{2,1,0:T(8,128)(2,1)S(1)}, u32[]{:S(2)}, u32[]{:S(2)}) collective-permute-start(bf16[32,8,256]{2,1,0:T(8,128)(2,1)} %get-tuple-element.20.own_ref), channel_id=1, source_target_pairs={{0,1},{1,0},{2,3},{3,2},{4,5},{5,4},{6,7},{7,6},{8,9},{9,8},{10,11... | collective-permute-start | bytes 393224 | tf_op jit(solution)/shard_map/ppermute | solution.py:318
  72.4 1.5 %collective-permute-done.2.far_ref = bf16[32,8,256]{2,1,0:T(8,128)(2,1)S(1)} collective-permute-done((bf16[32,8,256]{2,1,0:T(8,128)(2,1)}, bf16[32,8,256]{2,1,0:T(8,128)(2,1)S(1)}, u32[]{:S(2)}, u32[]{:S(2)}) %collective-permute-start.2) | collective-permute-done | bytes 131104 | tf_op jit(solution)/shard_map/ppermute | solution.py:318
  74.0 0.0 copy-start.3
  74.0 0.9 copy-done.3
  74.9 1.6 %landing.1 = (bf16[16,128]{1,0:T(8,128)(2,1)}, bf16[16,128]{1,0:T(8,128)(2,1)}) custom-call(s32[1,128]{1,0:T(1,128)} %bitcast.8, bf16[32,8,256]{2,1,0:T(8,128)(2,1)S(1)} %copy-done.3, bf16[32,8,256]{2,1,0:T(8,128)(2,1)S(1)} %collective-permute-done.2.far_ref), custom_call_target="tpu_custom_call" | custom-call | flops 4194304 | bytes 524288 | tf_op jit(solution)/shard_map/landing/pallas_call | solution.py:320
  76.5 8.8 %all-to-all-done.1.in_ref = bf16[16,8,1280]{2,1,0:T(8,128)(2,1)S(1)} async-done(((bf16[16,8,1280]{2,1,0:T(8,128)(2,1)}), bf16[16,8,1280]{2,1,0:T(8,128)(2,1)S(1)}, u32[]{:S(2)}, u32[]{:S(2)}) %all-to-all-start.1) | async-done | bytes 327712 | tf_op jit(solution)/shard_map/all_to_all | solution.py:252
  85.3 1.2 %project.1 = bf16[16,40,128]{2,1,0:T(8,128)(2,1)} custom-call(bf16[16,8,1280]{2,1,0:T(8,128)(2,1)S(1)} %all-to-all-done.1.in_ref, bf16[1024,256]{1,0:T(8,128)(2,1)S(1)} %copy-done, bf16[1024,256]{1,0:T(8,128)(2,1)S(1)} %collective-permute-done.1.far_ref), custom_call_target="tpu_custom_call" | custom-call | flops 167772160 | bytes 2097152 | tf_op jit(solution)/shard_map/project/pallas_call | solution.py:331
  86.5 11.9 %all_to_all.16.in_ref = bf16[16,40,128]{2,1,0:T(8,128)(2,1)S(1)} all-to-all(bf16[16,40,128]{2,1,0:T(8,128)(2,1)} %project.1), channel_id=1, replica_groups=mesh['seq_0'=4,'seq_1'=4,'pair'=2,'tensor'=8,'group'=2] {'pair','tensor'}, dimensions={0} | all-to-all | bytes 327680 | tf_op jit(solution)/shard_map/all_to_all | solution.py:252
  98.5 0.8 last.1
Async XLA Ops:
  0.6 4.0 %copy-start = (bf16[1024,256]{1,0:T(8,128)(2,1)S(1)}, bf16[1024,256]{1,0:T(8,128)(2,1)}, u32[]{:S(2)}) copy-start(bf16[1024,256]{1,0:T(8,128)(2,1)} %w_ref) | copy-start | bytes 1572868
  2.6 8.9 %copy-start.1 = (bf16[1024,128]{1,0:T(8,128)(2,1)S(1)}, bf16[1024,128]{1,0:T(8,128)(2,1)}, u32[]{:S(2)}) copy-start(bf16[1024,128]{1,0:T(8,128)(2,1)} %k_ref.3) | copy-start | bytes 786436
  2.6 9.0 %copy-start.2 = (bf16[1024,128]{1,0:T(8,128)(2,1)S(1)}, bf16[1024,128]{1,0:T(8,128)(2,1)}, u32[]{:S(2)}) copy-start(bf16[1024,128]{1,0:T(8,128)(2,1)} %v_ref.3) | copy-start | bytes 786436
  2.6 9.0 %copy-start.4 = (bf16[512,1024]{1,0:T(8,128)(2,1)S(1)}, bf16[512,1024]{1,0:T(8,128)(2,1)}, u32[]{:S(2)}) copy-start(bf16[512,1024]{1,0:T(8,128)(2,1)} %q_ref.3) | copy-start | bytes 3145732
  2.6 8.9 %collective-permute-start = (bf16[2064,128]{1,0:T(8,128)(2,1)}, bf16[2064,128]{1,0:T(8,128)(2,1)S(1)}, u32[]{:S(2)}, u32[]{:S(2)}) collective-permute-start(bf16[2064,128]{1,0:T(8,128)(2,1)} %pad_maximum_fusion), channel_id=1, source_target_pairs={{0,1},{1,0},{2,3},{3,2},{4,5},{5,4},{6,7},{7,6},{8,9},{9,8},{10,11... | collective-permute-start | bytes 1585160 | tf_op jit(solution)/shard_map/ppermute | solution.py:273
  4.7 16.2 %collective-permute-start.1 = (bf16[1024,256]{1,0:T(8,128)(2,1)S(1)}, bf16[1024,256]{1,0:T(8,128)(2,1)S(1)}, u32[]{:S(2)}, u32[]{:S(2)}) collective-permute-start(bf16[1024,256]{1,0:T(8,128)(2,1)S(1)} %copy-done), channel_id=1, source_target_pairs={{0,16},{16,0},{1,17},{17,1},{2,18},{18,2},{3,19},{19,3},{4,20},{20... | collective-permute-start | bytes 1572872 | tf_op jit(solution)/shard_map/ppermute | solution.py:272
  63.6 21.7 %all-to-all-start.1 = ((bf16[16,8,1280]{2,1,0:T(8,128)(2,1)}), bf16[16,8,1280]{2,1,0:T(8,128)(2,1)S(1)}, u32[]{:S(2)}, u32[]{:S(2)}) async-start(bf16[16,8,1280]{2,1,0:T(8,128)(2,1)} %get-tuple-element.19), calls=%async_computation.1 | async-start | bytes 655360 | tf_op jit(solution)/shard_map/all_to_all | solution.py:252
  70.5 3.5 %collective-permute-start.2 = (bf16[32,8,256]{2,1,0:T(8,128)(2,1)}, bf16[32,8,256]{2,1,0:T(8,128)(2,1)S(1)}, u32[]{:S(2)}, u32[]{:S(2)}) collective-permute-start(bf16[32,8,256]{2,1,0:T(8,128)(2,1)} %get-tuple-element.20.own_ref), channel_id=1, source_target_pairs={{0,1},{1,0},{2,3},{3,2},{4,5},{5,4},{6,7},{7,6},{8,9},{9,8},{10,11... | collective-permute-start | bytes 393224 | tf_op jit(solution)/shard_map/ppermute | solution.py:318
  74.0 0.9 copy-start.3

commit v6 on v5

--- a/solution.py
+++ b/solution.py
@@ -114,14 +114,12 @@
     first = jnp.full((8, HEAD), group, jnp.int32) == 0
     near_k = jnp.concatenate([jnp.where(first, own_k, far_k), jnp.where(first, far_k, own_k)], axis=0)
     near_v = jnp.concatenate([jnp.where(first, own_v, far_v), jnp.where(first, far_v, own_v)], axis=0)
-    keys[0:CACHED, :] = k_ref[...]
-    keys[CACHED : 2 * CACHED, :] = other_ref[0:CACHED, :]
     values[:, HEAD:] = jnp.ones((KEYS, HEAD), bf16)
     values[0:CACHED, 0:HEAD] = v_ref[...]
     values[CACHED : 2 * CACHED, 0:HEAD] = other_ref[CACHED : 2 * CACHED, :]
-    keys[2 * CACHED :, :] = jnp.zeros((HEAD, HEAD), bf16)
+    keys[...] = jnp.zeros((HEAD, HEAD), bf16)
     values[2 * CACHED :, 0:HEAD] = jnp.zeros((HEAD, HEAD), bf16)
-    keys[2 * CACHED : 2 * CACHED + 16, :] = near_k.astype(bf16)
+    keys[0:16, :] = near_k.astype(bf16)
     values[2 * CACHED : 2 * CACHED + 16, 0:HEAD] = near_v.astype(bf16)
     for a in range(2):
         out_ref[:, a, :, DEC:NEW] = dec_ref[:, a, :, 0 : 2 * HEAD]
@@ -135,8 +133,9 @@
     mine = pl.ds(pl.multiple_of(group * HALF, HALF), HALF)
 
     def scores(h):
-        s = dot_t(q_ref[mine, h * HEAD : (h + 1) * HEAD], keys[...])
-        return jnp.concatenate([s[:, : 2 * CACHED], jnp.where(seen, s[:, 2 * CACHED :], NEG)], axis=1)
+        q = q_ref[mine, h * HEAD : (h + 1) * HEAD]
+        edge = jnp.where(seen, dot_t(q, keys[...]), NEG)
+        return jnp.concatenate([dot_t(q, k_ref[...]), dot_t(q, other_ref[0:CACHED, :]), edge], axis=1)
 
     upcoming = scores(0)
     stat = jnp.concatenate([dec_ref[:, a, :, 2 * HEAD :].astype(f32) for a in range(2)], axis=0)
@@ -289,7 +288,7 @@
         out_shape=jax.ShapeDtypeStruct((MATES, 2, 8, WIDE), bf16),
         in_specs=[VMEM] * 7,
         out_specs=VMEM,
-        scratch_shapes=[pltpu.VMEM((KEYS, HEAD), bf16), pltpu.VMEM((KEYS, 2 * HEAD), bf16)],
+        scratch_shapes=[pltpu.VMEM((HEAD, HEAD), bf16), pltpu.VMEM((KEYS, 2 * HEAD), bf16)],
         cost_estimate=cost(4 * HALF * LOCAL * KEYS * HEAD, 4 << 20, HALF * LOCAL * KEYS),
     )(
         near(prefill_queries),

time: 99.8 us -> 99.8 us (level)
  no operation moved by 1% of the time
where the time goes in v6:
time: 99.8 us; the launch traced here: 99.2 us
  blocking collectives  53.4 us (54%)
  Pallas kernels  16 us (16%)
  starting transfers between devices  14.3 us (14%)
  waiting for transfers between devices  11.9 us (12%)
  other arithmetic  1.96 us (2%)
    all_to_all x2, blocking collectives, swap(): return lax.all_to_all(x, axis, 0, 0, tiled=True)  53.4 us
    all_to_all x1, waiting for transfers between devices, swap(): return lax.all_to_all(x, axis, 0, 0, tiled=True)  8.83 us
    pallas_call x1, Pallas kernels, body(): pl.pallas_call(prefill_kernel, name='prefill', out_shape=jax.ShapeDtypeSt...  7.74 us
    all_to_all x1, starting transfers between devices, swap(): return lax.all_to_all(x, axis, 0, 0, tiled=True)  6.86 us
    ppermute x1, starting transfers between devices, body(): far_weight = lax.ppermute(out_weight, 'pair', [(0, 1), (1, 0)])  3.48 us
    pallas_call x1, Pallas kernels, body(): pl.pallas_call(decode_kernel, name='decode', out_shape=jax.ShapeDtypeStru...  3.38 us
    ppermute x1, starting transfers between devices, body(): other = lax.ppermute(mine, 'group', [(0, 1), (1, 0)])  2.05 us
  transfers between devices with their start and end apart: 4, of which 3 were waited for; matrix products, arithmetic and copies ran while one was open for 0% of the time, Pallas kernels for 13%

profile of v6, /device:TPU:2, one launch (start us, length us, event | category | flops | bytes accessed | tf_op | source)
XLA Modules:
  0.0 99.2 jit_solution(16465341312763733375)
XLA Ops:
  0.6 0.0 copy-start
  0.6 2.0 %pad_maximum_fusion = bf16[2064,128]{1,0:T(8,128)(2,1)} fusion(bf16[8,128]{1,0:T(8,128)(2,1)} %sv_ref.1, bf16[8,128]{1,0:T(8,128)(2,1)} %sk_ref.1, bf16[1024,128]{1,0:T(8,128)(2,1)} %v_ref.3, bf16[1024,128]{1,0:T(8,128)(2,1)} %k_ref.3), kind=kLoop, calls=%fused_computation | loop fusion | flops 2113536 | bytes 1056768 | tf_op jit(solution)/shard_map/concatenate | solution.py:270
  2.6 0.0 copy-start.1
  2.6 0.0 copy-start.2
  2.6 0.0 copy-start.4
  2.6 2.0 %collective-permute-start = (bf16[2064,128]{1,0:T(8,128)(2,1)}, bf16[2064,128]{1,0:T(8,128)(2,1)S(1)}, u32[]{:S(2)}, u32[]{:S(2)}) collective-permute-start(bf16[2064,128]{1,0:T(8,128)(2,1)} %pad_maximum_fusion), channel_id=1, source_target_pairs={{0,1},{1,0},{2,3},{3,2},{4,5},{5,4},{6,7},{7,6},{8,9},{9,8},{10,11... | collective-permute-start | bytes 1585160 | tf_op jit(solution)/shard_map/ppermute | solution.py:272
  4.7 0.0 copy-done
  4.7 3.5 %collective-permute-start.1 = (bf16[1024,256]{1,0:T(8,128)(2,1)S(1)}, bf16[1024,256]{1,0:T(8,128)(2,1)S(1)}, u32[]{:S(2)}, u32[]{:S(2)}) collective-permute-start(bf16[1024,256]{1,0:T(8,128)(2,1)S(1)} %copy-done), channel_id=1, source_target_pairs={{0,16},{16,0},{1,17},{17,1},{2,18},{18,2},{3,19},{19,3},{4,20},{20... | collective-permute-start | bytes 1572872 | tf_op jit(solution)/shard_map/ppermute | solution.py:271
  8.2 3.4 %decode.1 = bf16[32,8,384]{2,1,0:T(8,128)(2,1)} custom-call(s32[32]{0:T(128)} %lengths.1, s32[16]{0:T(128)} %requests.1, bf16[4,16,1024]{2,1,0:T(8,128)(2,1)} %q_ref.2, bf16[16,256,128]{2,1,0:T(8,128)(2,1)} %k_ref.2, bf16[16,256,128]{2,1,0:T(8,128)(2,1)} %v_ref.2, bf16[4,16,128]{2,1,0:T(8,128)(2,1)} %nk_ref.1, bf16[4,16,128]{2,1,0:T(8,128)(2,1)} %nv_ref.1), custom_call_target="tpu_custom_call" | custom-call | flops 536870912 | bytes 3145728 | tf_op jit(solution)/shard_map/decode/pallas_call | solution.py:275
  11.5 0.0 collective-permute-done.other_ref
  11.5 0.0 copy-done.1
  11.6 0.0 copy-done.2
  11.6 0.0 copy-done.4
  11.6 7.7 %prefill.1 = bf16[16,2,8,1664]{3,2,1,0:T(8,128)(2,1)} custom-call(bf16[512,1024]{1,0:T(8,128)(2,1)S(1)} %copy-done.4, bf16[1024,128]{1,0:T(8,128)(2,1)S(1)} %copy-done.1, bf16[1024,128]{1,0:T(8,128)(2,1)S(1)} %copy-done.2, bf16[8,128]{1,0:T(8,128)(2,1)} %sk_ref.1, bf16[8,128]{1,0:T(8,128)(2,1)} %sv_ref.1, ...), custom_call_target="tpu_custom_call" | custom-call | flops 2281701376 | bytes 4194304 | tf_op jit(solution)/shard_map/prefill/pallas_call | solution.py:285
  19.3 1.6 %collective-permute-done.1.far_ref = bf16[1024,256]{1,0:T(8,128)(2,1)S(1)} collective-permute-done((bf16[1024,256]{1,0:T(8,128)(2,1)S(1)}, bf16[1024,256]{1,0:T(8,128)(2,1)S(1)}, u32[]{:S(2)}, u32[]{:S(2)}) %collective-permute-start.1) | collective-permute-done | bytes 524320 | tf_op jit(solution)/shard_map/ppermute | solution.py:271
  20.9 41.4 %all_to_all.15.in_ref = bf16[32,8,1664]{2,1,0:T(8,128)(2,1)S(1)} all-to-all(bf16[32,8,1664]{2,1,0:T(8,128)(2,1)} %bitcast.6), channel_id=1, replica_groups=mesh['seq_0'=4,'seq_1'=4,'pair'=2,'tensor'=8,'group'=2] {'seq_0','seq_1'..., dimensions={0} | all-to-all | bytes 1703936 | tf_op jit(solution)/shard_map/all_to_all | solution.py:251
  62.3 1.3 %combine.1 = (bf16[16,8,1280]{2,1,0:T(8,128)(2,1)}, bf16[32,8,256]{2,1,0:T(8,128)(2,1)}) custom-call(bf16[32,8,1664]{2,1,0:T(8,128)(2,1)S(1)} %all_to_all.15.in_ref), custom_call_target="tpu_custom_call" | custom-call | flops 1048576 | bytes 2097152 | tf_op jit(solution)/shard_map/combine/pallas_call | solution.py:306
  63.6 6.9 %all-to-all-start.1 = ((bf16[16,8,1280]{2,1,0:T(8,128)(2,1)}), bf16[16,8,1280]{2,1,0:T(8,128)(2,1)S(1)}, u32[]{:S(2)}, u32[]{:S(2)}) async-start(bf16[16,8,1280]{2,1,0:T(8,128)(2,1)} %get-tuple-element.19), calls=%async_computation.1 | async-start | bytes 655360 | tf_op jit(solution)/shard_map/all_to_all | solution.py:251
  70.5 1.9 %collective-permute-start.2 = (bf16[32,8,256]{2,1,0:T(8,128)(2,1)}, bf16[32,8,256]{2,1,0:T(8,128)(2,1)S(1)}, u32[]{:S(2)}, u32[]{:S(2)}) collective-permute-start(bf16[32,8,256]{2,1,0:T(8,128)(2,1)} %get-tuple-element.20.own_ref), channel_id=1, source_target_pairs={{0,1},{1,0},{2,3},{3,2},{4,5},{5,4},{6,7},{7,6},{8,9},{9,8},{10,11... | collective-permute-start | bytes 393224 | tf_op jit(solution)/shard_map/ppermute | solution.py:317
  72.4 1.5 %collective-permute-done.2.far_ref = bf16[32,8,256]{2,1,0:T(8,128)(2,1)S(1)} collective-permute-done((bf16[32,8,256]{2,1,0:T(8,128)(2,1)}, bf16[32,8,256]{2,1,0:T(8,128)(2,1)S(1)}, u32[]{:S(2)}, u32[]{:S(2)}) %collective-permute-start.2) | collective-permute-done | bytes 131104 | tf_op jit(solution)/shard_map/ppermute | solution.py:317
  74.0 0.0 copy-start.3
  74.0 0.9 copy-done.3
  74.9 1.6 %landing.1 = (bf16[16,128]{1,0:T(8,128)(2,1)}, bf16[16,128]{1,0:T(8,128)(2,1)}) custom-call(s32[1,128]{1,0:T(1,128)} %bitcast.8, bf16[32,8,256]{2,1,0:T(8,128)(2,1)S(1)} %copy-done.3, bf16[32,8,256]{2,1,0:T(8,128)(2,1)S(1)} %collective-permute-done.2.far_ref), custom_call_target="tpu_custom_call" | custom-call | flops 4194304 | bytes 524288 | tf_op jit(solution)/shard_map/landing/pallas_call | solution.py:319
  76.5 8.8 %all-to-all-done.1.in_ref = bf16[16,8,1280]{2,1,0:T(8,128)(2,1)S(1)} async-done(((bf16[16,8,1280]{2,1,0:T(8,128)(2,1)}), bf16[16,8,1280]{2,1,0:T(8,128)(2,1)S(1)}, u32[]{:S(2)}, u32[]{:S(2)}) %all-to-all-start.1) | async-done | bytes 327712 | tf_op jit(solution)/shard_map/all_to_all | solution.py:251
  85.3 1.2 %project.1 = bf16[16,40,128]{2,1,0:T(8,128)(2,1)} custom-call(bf16[16,8,1280]{2,1,0:T(8,128)(2,1)S(1)} %all-to-all-done.1.in_ref, bf16[1024,256]{1,0:T(8,128)(2,1)S(1)} %copy-done, bf16[1024,256]{1,0:T(8,128)(2,1)S(1)} %collective-permute-done.1.far_ref), custom_call_target="tpu_custom_call" | custom-call | flops 167772160 | bytes 2097152 | tf_op jit(solution)/shard_map/project/pallas_call | solution.py:330
  86.5 11.9 %all_to_all.16.in_ref = bf16[16,40,128]{2,1,0:T(8,128)(2,1)S(1)} all-to-all(bf16[16,40,128]{2,1,0:T(8,128)(2,1)} %project.1), channel_id=1, replica_groups=mesh['seq_0'=4,'seq_1'=4,'pair'=2,'tensor'=8,'group'=2] {'pair','tensor'}, dimensions={0} | all-to-all | bytes 327680 | tf_op jit(solution)/shard_map/all_to_all | solution.py:251
  98.5 0.8 last.1
Async XLA Ops:
  0.6 4.0 %copy-start = (bf16[1024,256]{1,0:T(8,128)(2,1)S(1)}, bf16[1024,256]{1,0:T(8,128)(2,1)}, u32[]{:S(2)}) copy-start(bf16[1024,256]{1,0:T(8,128)(2,1)} %w_ref) | copy-start | bytes 1572868
  2.6 8.9 %copy-start.1 = (bf16[1024,128]{1,0:T(8,128)(2,1)S(1)}, bf16[1024,128]{1,0:T(8,128)(2,1)}, u32[]{:S(2)}) copy-start(bf16[1024,128]{1,0:T(8,128)(2,1)} %k_ref.3) | copy-start | bytes 786436
  2.6 9.0 %copy-start.2 = (bf16[1024,128]{1,0:T(8,128)(2,1)S(1)}, bf16[1024,128]{1,0:T(8,128)(2,1)}, u32[]{:S(2)}) copy-start(bf16[1024,128]{1,0:T(8,128)(2,1)} %v_ref.3) | copy-start | bytes 786436
  2.6 9.0 %copy-start.4 = (bf16[512,1024]{1,0:T(8,128)(2,1)S(1)}, bf16[512,1024]{1,0:T(8,128)(2,1)}, u32[]{:S(2)}) copy-start(bf16[512,1024]{1,0:T(8,128)(2,1)} %q_ref.3) | copy-start | bytes 3145732
  2.6 8.9 %collective-permute-start = (bf16[2064,128]{1,0:T(8,128)(2,1)}, bf16[2064,128]{1,0:T(8,128)(2,1)S(1)}, u32[]{:S(2)}, u32[]{:S(2)}) collective-permute-start(bf16[2064,128]{1,0:T(8,128)(2,1)} %pad_maximum_fusion), channel_id=1, source_target_pairs={{0,1},{1,0},{2,3},{3,2},{4,5},{5,4},{6,7},{7,6},{8,9},{9,8},{10,11... | collective-permute-start | bytes 1585160 | tf_op jit(solution)/shard_map/ppermute | solution.py:272
  4.7 16.2 %collective-permute-start.1 = (bf16[1024,256]{1,0:T(8,128)(2,1)S(1)}, bf16[1024,256]{1,0:T(8,128)(2,1)S(1)}, u32[]{:S(2)}, u32[]{:S(2)}) collective-permute-start(bf16[1024,256]{1,0:T(8,128)(2,1)S(1)} %copy-done), channel_id=1, source_target_pairs={{0,16},{16,0},{1,17},{17,1},{2,18},{18,2},{3,19},{19,3},{4,20},{20... | collective-permute-start | bytes 1572872 | tf_op jit(solution)/shard_map/ppermute | solution.py:271
  63.6 21.7 %all-to-all-start.1 = ((bf16[16,8,1280]{2,1,0:T(8,128)(2,1)}), bf16[16,8,1280]{2,1,0:T(8,128)(2,1)S(1)}, u32[]{:S(2)}, u32[]{:S(2)}) async-start(bf16[16,8,1280]{2,1,0:T(8,128)(2,1)} %get-tuple-element.19), calls=%async_computation.1 | async-start | bytes 655360 | tf_op jit(solution)/shard_map/all_to_all | solution.py:251
  70.5 3.5 %collective-permute-start.2 = (bf16[32,8,256]{2,1,0:T(8,128)(2,1)}, bf16[32,8,256]{2,1,0:T(8,128)(2,1)S(1)}, u32[]{:S(2)}, u32[]{:S(2)}) collective-permute-start(bf16[32,8,256]{2,1,0:T(8,128)(2,1)} %get-tuple-element.20.own_ref), channel_id=1, source_target_pairs={{0,1},{1,0},{2,3},{3,2},{4,5},{5,4},{6,7},{7,6},{8,9},{9,8},{10,11... | collective-permute-start | bytes 393224 | tf_op jit(solution)/shard_map/ppermute | solution.py:317
  74.0 0.9 copy-start.3
